TPU v7x, 128 devices: a whole 4x4x4 slice. The times are simulated.
128 devices in a mesh: dp: 16 (over x, z), seq: 8 (over y, core).
Axes of the slice: x: 4, y: 4, z: 4, core: 2. Of those that a mesh axis runs over, the one named last changes fastest.
Arguments:
- grad_out: bfloat16 [16, 1024, 4096], P('dp', 'seq'), may hold values from -6 to 6
- queries: bfloat16 [16, 1024, 4096], P('dp', 'seq'), may hold values from -45 to 45
- keys: bfloat16 [16, 1024, 1024], P('dp', 'seq'), may hold values from -4 to 4
- values: bfloat16 [16, 1024, 1024], P('dp', 'seq'), may hold values from -6 to 6
- out_weight: bfloat16 [4096, 4096], P('seq'), may hold values from -0.09375 to 0.09375
- doc_starts: int32 [16, 8], P('dp'), may hold values from 0 to 1020, as said below
Outputs:
- grad_queries: bfloat16 [16, 1024, 4096], P('dp', 'seq')
- grad_keys: bfloat16 [16, 1024, 1024], P('dp', 'seq')
- grad_values: bfloat16 [16, 1024, 1024], P('dp', 'seq')
- grad_weight: float32 [4096, 4096], P('seq', 'dp')
Inputs may be any that keep to these rules, and one draw needn't show every extreme that they name: `doc_starts`: each row strictly increases, holds multiples of 4, begins with 0 and ends with 1020.
All inputs are finite; a program needn't handle non-finite values.
Results may differ from a plain program's by a relative error of at most 0.015.
Values may be sent and summed in bfloat16 or wider, within the bound.
A program may use at most 128 MiB of HBM per device.

v0:
```python
import math

import jax
import jax.numpy as jnp
from jax import lax
from jax.sharding import PartitionSpec as P

HEADS = 32
KV_HEADS = 8
HEAD_DIM = 128


def visible(starts, first_row, row_count, key_count):
    rows_pos = first_row + jnp.arange(row_count, dtype=jnp.int32)
    keys_pos = jnp.arange(key_count, dtype=jnp.int32)
    opening = jnp.max(jnp.where(starts[None, :] <= rows_pos[:, None], starts[None, :], 0), axis=1)
    return (keys_pos[None, :] >= opening[:, None]) & (keys_pos[None, :] <= rows_pos[:, None])


def weights_of(query_rows, key_rows, allowed, scale):
    scores = (
        lax.dot_general(
            query_rows, key_rows, (((1,), (1,)), ((), ())), preferred_element_type=jnp.float32
        )
        * scale
    )
    scores = jnp.where(allowed, scores, -1e30)
    highest = jnp.max(scores, axis=1, keepdims=True)
    raised = jnp.exp(scores - highest)
    return raised / jnp.sum(raised, axis=1, keepdims=True)


def attend(query_all, key_all, value_all, starts, head_dim, block):
    length = query_all.shape[0]
    scale = 1.0 / math.sqrt(head_dim)
    columns = []
    for member in range(query_all.shape[1] // head_dim):
        query_head = query_all[:, member * head_dim : (member + 1) * head_dim]
        blocks = []
        for section in range(length // block):
            first = section * block
            ending = first + block
            allowed = visible(starts, first, block, ending)
            probs = weights_of(query_head[first : first + block], key_all[:ending], allowed, scale)
            blocks.append(
                jnp.dot(
                    probs.astype(jnp.bfloat16),
                    value_all[:ending],
                    preferred_element_type=jnp.float32,
                ).astype(jnp.bfloat16)
            )
        columns.append(jnp.concatenate(blocks, axis=0))
    return jnp.concatenate(columns, axis=1)


def attend_back(query_all, key_all, value_all, out_all, grad_all, starts, group, head_dim, block):
    length = query_all.shape[0]
    scale = 1.0 / math.sqrt(head_dim)
    key_grads = [jnp.zeros((length, head_dim), jnp.float32)]
    value_grads = [jnp.zeros((length, head_dim), jnp.float32)]
    query_grads = []
    for member in range(query_all.shape[1] // head_dim):
        shared = member // group
        lo_col = member * head_dim
        query_head = query_all[:, lo_col : lo_col + head_dim]
        blocks = []
        for section in range(length // block):
            first = section * block
            ending = first + block
            allowed = visible(starts, first, block, ending)
            query_rows = query_head[first : first + block]
            probs = weights_of(query_rows, key_all[:ending], allowed, scale)
            probs_low = probs.astype(jnp.bfloat16)
            grad_rows = grad_all[first : first + block, lo_col : lo_col + head_dim]
            out_rows = out_all[first : first + block, lo_col : lo_col + head_dim]
            value_grads[shared] = (
                value_grads[shared]
                .at[:ending]
                .add(
                    lax.dot_general(
                        probs_low,
                        grad_rows,
                        (((0,), (0,)), ((), ())),
                        preferred_element_type=jnp.float32,
                    )
                )
            )
            grad_probs = lax.dot_general(
                grad_rows,
                value_all[:ending],
                (((1,), (1,)), ((), ())),
                preferred_element_type=jnp.float32,
            )
            delta = jnp.sum(
                grad_rows.astype(jnp.float32) * out_rows.astype(jnp.float32), axis=1, keepdims=True
            )
            grad_scores = (probs * (grad_probs - delta)).astype(jnp.bfloat16)
            blocks.append(
                (
                    jnp.dot(grad_scores, key_all[:ending], preferred_element_type=jnp.float32)
                    * scale
                ).astype(jnp.bfloat16)
            )
            key_grads[shared] = (
                key_grads[shared]
                .at[:ending]
                .add(
                    lax.dot_general(
                        grad_scores,
                        query_rows,
                        (((0,), (0,)), ((), ())),
                        preferred_element_type=jnp.float32,
                    )
                    * scale
                )
            )
        query_grads.append(jnp.concatenate(blocks, axis=0))
    grad_q = jnp.concatenate(query_grads, axis=1)
    grad_k = key_grads[0].astype(jnp.bfloat16)
    grad_v = value_grads[0].astype(jnp.bfloat16)
    return (grad_q, grad_k, grad_v)


def body(grad_out, queries, keys, values, out_weight, doc_starts):
    cotangent = grad_out[0]
    starts = doc_starts[0]
    query_heads, key_heads, value_heads = (
        lax.all_to_all(queries[0], "seq", split_axis=1, concat_axis=0, tiled=True),
        lax.all_to_all(keys[0], "seq", split_axis=1, concat_axis=0, tiled=True),
        lax.all_to_all(values[0], "seq", split_axis=1, concat_axis=0, tiled=True),
    )
    length = query_heads.shape[0]
    group = HEADS // KV_HEADS
    block = min(512, length)
    out_all = attend(query_heads, key_heads, value_heads, starts, HEAD_DIM, block)
    piece = lax.all_gather(cotangent, "seq", axis=0, tiled=True)
    projected = lax.dot_general(
        piece, out_weight, (((1,), (1,)), ((), ())), preferred_element_type=jnp.float32
    )
    grad_acc = projected
    weight_acc = lax.dot_general(
        out_all, piece, (((0,), (0,)), ((), ())), preferred_element_type=jnp.float32
    )
    grad_acc, weight_acc = (grad_acc, weight_acc)
    grad_attn = grad_acc.astype(jnp.bfloat16)
    weight_part = lax.psum_scatter(
        weight_acc.astype(jnp.bfloat16), "dp", scatter_dimension=1, tiled=True
    ).astype(jnp.float32)
    weight_grad = weight_part * (1.0 / math.sqrt(length * lax.axis_size("dp")))
    grad_q, grad_k, grad_v = attend_back(
        query_heads, key_heads, value_heads, out_all, grad_attn, starts, group, HEAD_DIM, block
    )
    back_q, back_k, back_v = (
        lax.all_to_all(grad_q, "seq", split_axis=0, concat_axis=1, tiled=True),
        lax.all_to_all(grad_k, "seq", split_axis=0, concat_axis=1, tiled=True),
        lax.all_to_all(grad_v, "seq", split_axis=0, concat_axis=1, tiled=True),
    )
    return (back_q[None], back_k[None], back_v[None], weight_grad)


def solution(mesh):
    return jax.shard_map(
        body,
        mesh=mesh,
        in_specs=(
            P("dp", "seq", None),
            P("dp", "seq", None),
            P("dp", "seq", None),
            P("dp", "seq", None),
            P("seq", None),
            P("dp", None),
        ),
        out_specs=(
            P("dp", "seq", None),
            P("dp", "seq", None),
            P("dp", "seq", None),
            P("seq", "dp"),
        ),
        check_vma=False,
    )
```

profile of v0, /device:TPU:1, one launch (start us, length us, event | category | flops | bytes accessed | tf_op | source)
XLA Modules:
  0.0 202.4 jit_solution(4503599995519726671)
XLA Ops:
  7.2 0.7 all-gather.3.cloned.1.call-update
  7.9 1.8 copy.65
  9.7 6.0 %all-to-all-start.1 = ((bf16[128,8,128]{0,2,1:T(8,128)(2,1)}), bf16[128,8,128]{0,2,1:T(8,128)(2,1)S(1)}, u32[]{:S(2)}, u32[]{:S(2)}) async-start(bf16[128,8,128]{0,2,1:T(8,128)(2,1)} %bitcast.4), calls=%async_computation.1 | async-start | bytes 524288 | tf_op jit(solution)/shard_map/all_to_all | solution.py:129
  15.7 0.8 copy.67
  16.5 5.6 %all-to-all-done.1 = bf16[128,8,128]{0,2,1:T(8,128)(2,1)S(1)} async-done(((bf16[128,8,128]{0,2,1:T(8,128)(2,1)}), bf16[128,8,128]{0,2,1:T(8,128)(2,1)S(1)}, u32[]{:S(2)}, u32[]{:S(2)}) %all-to-all-start.1) | async-done | bytes 262176 | tf_op jit(solution)/shard_map/all_to_all | solution.py:129
  22.1 4.4 %all-to-all-start.2 = ((bf16[128,8,128]{0,2,1:T(8,128)(2,1)}), bf16[128,8,128]{0,2,1:T(8,128)(2,1)S(1)}, u32[]{:S(2)}, u32[]{:S(2)}) async-start(bf16[128,8,128]{0,2,1:T(8,128)(2,1)} %bitcast.8), calls=%async_computation.2 | async-start | bytes 524288 | tf_op jit(solution)/shard_map/all_to_all | solution.py:130
  26.5 1.3 copy.63
  27.8 8.6 %all-to-all-done.2 = bf16[128,8,128]{0,2,1:T(8,128)(2,1)S(1)} async-done(((bf16[128,8,128]{0,2,1:T(8,128)(2,1)}), bf16[128,8,128]{0,2,1:T(8,128)(2,1)S(1)}, u32[]{:S(2)}, u32[]{:S(2)}) %all-to-all-start.2) | async-done | bytes 262176 | tf_op jit(solution)/shard_map/all_to_all | solution.py:130
  36.4 4.3 %all-to-all-start = ((bf16[128,8,512]{0,2,1:T(8,128)(2,1)}), bf16[128,8,512]{0,2,1:T(8,128)(2,1)S(1)}, u32[]{:S(2)}, u32[]{:S(2)}) async-start(bf16[128,8,512]{0,2,1:T(8,128)(2,1)} %bitcast.1), calls=%async_computation | async-start | bytes 2097152 | tf_op jit(solution)/shard_map/all_to_all | solution.py:128
  41.5 26.0 %all-to-all-done = bf16[128,8,512]{0,2,1:T(8,128)(2,1)S(1)} async-done(((bf16[128,8,512]{0,2,1:T(8,128)(2,1)}), bf16[128,8,512]{0,2,1:T(8,128)(2,1)S(1)}, u32[]{:S(2)}, u32[]{:S(2)}) %all-to-all-start) | async-done | bytes 1048608 | tf_op jit(solution)/shard_map/all_to_all | solution.py:128
  67.5 1.3 copy.64
  68.8 1.3 fusion.127
  72.1 1.1 fusion.124
  73.7 1.1 fusion.126
  75.3 1.1 fusion.128
  76.8 1.3 fusion.130
  78.8 0.8 copy-done.21
  79.6 0.9 convolution_convert_fusion.2
  80.7 0.8 copy-done.19
  81.5 0.9 convolution_convert_fusion.1
  82.6 0.9 convolution_convert_fusion
  83.6 1.0 fusion.89
  85.0 1.3 copy-done.6
  86.3 1.2 convolution_convert_fusion.7
  88.0 1.3 copy-done.3
  89.3 1.2 convolution_convert_fusion.6
  91.0 1.4 convolution_convert_fusion.5
  92.8 1.1 convolution_convert_fusion.4
  94.1 9.2 %fusion.16 = bf16[1024,512]{0,1:T(8,128)(2,1)S(1)} fusion(bf16[512,4096]{1,0:T(8,128)(2,1)} %param.58, bf16[1,1024,4096]{2,1,0:T(8,128)(2,1)} %all-gather.3.cloned.1.call-done), kind=kOutput, calls=%fused_computation.28 | convolution fusion | flops 4295491584 | bytes 13631488 | tf_op jit(solution)/shard_map/dot_general | solution.py:137
  103.4 1.1 multiply_reduce_fusion.7
  104.5 1.1 fusion.29
  105.6 0.7 copy-done.7
  107.4 0.8 copy-done.35
  108.2 1.9 convolution_multiply_fusion.11
  110.1 6.1 %fusion.4 = bf16[512,4096]{1,0:T(8,128)(2,1)} fusion(bf16[1,1024,4096]{2,1,0:T(8,128)(2,1)S(1)} %copy-done.70, bf16[512,128]{0,1:T(8,128)(2,1)S(1)} %copy-done.54, bf16[512,128]{0,1:T(8,128)(2,1)S(1)} %copy-done.57, bf16[512,128]{0,1:T(8,128)(2,1)S(1)} %copy-done.53, bf16[512,128]{0,1:T(8,128)(2,1)S(1)} %copy-done.56, bf16[512,128]{0,1:T(8,128)(2,1)S(1)} %copy-done.52, ...), kind=kOutput, calls=%fused_computation.4 | convolution fusion | flops 4305453056 | bytes 13631488 | tf_op jit(solution)/shard_map/dot_general | solution.py:141
  116.2 1.6 fusion.31
  117.9 1.4 fusion.41
  119.6 1.4 copy-done.4
  122.4 0.8 copy-done.24
  123.6 1.4 copy-done.1
  126.9 1.2 fusion.35
  128.1 4.8 %all-to-all-start.4 = ((bf16[8,128,128]{2,1,0:T(8,128)(2,1)}), bf16[8,128,128]{2,1,0:T(8,128)(2,1)}, u32[]{:S(2)}, u32[]{:S(2)}) async-start(bf16[8,128,128]{2,1,0:T(8,128)(2,1)} %bitcast.15), calls=%async_computation.4 | async-start | bytes 524288 | tf_op jit(solution)/shard_map/all_to_all | solution.py:155
  132.8 2.2 %fusion.49 = bf16[512,128]{1,0:T(8,128)(2,1)} fusion(bf16[512,512]{0,1:T(8,128)(2,1)} %copy-done.39, bf16[512,128]{1,0:T(8,128)(2,1)S(1)} %bitcast.122), kind=kOutput, calls=%fused_computation.90 | convolution fusion | flops 67239936 | bytes 786432 | tf_op jit(solution)/shard_map/dot_general | solution.py:100
  135.0 2.1 %fusion.48 = bf16[512,128]{1,0:T(8,128)(2,1)} fusion(bf16[512,512]{0,1:T(8,128)(2,1)} %copy-done.38, bf16[512,128]{1,0:T(8,128)(2,1)S(1)} %bitcast.123), kind=kOutput, calls=%fused_computation.89 | convolution fusion | flops 67239936 | bytes 786432 | tf_op jit(solution)/shard_map/dot_general | solution.py:100
  137.1 1.5 fusion.120
  138.6 1.5 convolution_add_fusion.3
  141.5 0.6 copy-done.2
  143.5 1.1 fusion.53
  144.6 1.1 fusion.52
  145.7 1.1 fusion.51
  146.8 1.1 fusion.50
  147.9 1.2 fusion.36
  149.5 4.8 %all-to-all-start.5 = ((bf16[8,128,128]{2,1,0:T(8,128)(2,1)}), bf16[8,128,128]{2,1,0:T(8,128)(2,1)S(1)}, u32[]{:S(2)}, u32[]{:S(2)}) async-start(bf16[8,128,128]{2,1,0:T(8,128)(2,1)} %bitcast.17), calls=%async_computation.5 | async-start | bytes 524288 | tf_op jit(solution)/shard_map/all_to_all | solution.py:156
  154.7 1.1 maximum_maximum_fusion
  155.8 5.0 %all-to-all-done.5 = bf16[8,128,128]{2,1,0:T(8,128)(2,1)S(1)} async-done(((bf16[8,128,128]{2,1,0:T(8,128)(2,1)}), bf16[8,128,128]{2,1,0:T(8,128)(2,1)S(1)}, u32[]{:S(2)}, u32[]{:S(2)}) %all-to-all-start.5) | async-done | bytes 262176 | tf_op jit(solution)/shard_map/all_to_all | solution.py:156
  160.7 4.5 %all-to-all-start.3 = ((bf16[8,128,512]{2,1,0:T(8,128)(2,1)}), bf16[8,128,512]{2,1,0:T(8,128)(2,1)S(1)}, u32[]{:S(2)}, u32[]{:S(2)}) async-start(bf16[8,128,512]{2,1,0:T(8,128)(2,1)} %bitcast.13), calls=%async_computation.3 | async-start | bytes 2097152 | tf_op jit(solution)/shard_map/all_to_all | solution.py:154
  165.2 1.1 copy.84
  166.4 0.8 broadcast_in_dim.102
  167.4 0.8 broadcast_in_dim.103
  168.2 12.1 %all-to-all-done.3 = bf16[8,128,512]{2,1,0:T(8,128)(2,1)S(1)} async-done(((bf16[8,128,512]{2,1,0:T(8,128)(2,1)}), bf16[8,128,512]{2,1,0:T(8,128)(2,1)S(1)}, u32[]{:S(2)}, u32[]{:S(2)}) %all-to-all-start.3) | async-done | bytes 1048608 | tf_op jit(solution)/shard_map/all_to_all | solution.py:154
  180.2 0.6 copy.83
  180.8 1.3 broadcast_in_dim.101
  182.1 11.6 %reduce-scatter.2.cloned.1.call-done = bf16[512,256]{1,0:T(8,128)(2,1)} async-done(((bf16[512,4096]{1,0:T(8,128)(2,1)}), bf16[512,256]{1,0:T(8,128)(2,1)}) %reduce-scatter.2.cloned.1.call-update) | async-done | bytes 262160 | tf_op jit(solution)/shard_map/reduce_scatter | solution.py:146
  193.8 1.8 convert_multiply_fusion
  (186 shorter events, 15.6 us)
Async XLA Ops:
  7.2 8.5 %copy-start.50 = (bf16[1,128,1024]{2,1,0:T(8,128)(2,1)S(1)}, bf16[1,128,1024]{2,1,0:T(8,128)(2,1)}, u32[]{:S(2)}) copy-start(bf16[1,128,1024]{2,1,0:T(8,128)(2,1)} %param.57) | copy-start | bytes 786436
  7.2 19.3 %copy-start.43 = (bf16[1,128,4096]{2,1,0:T(8,128)(2,1)S(1)}, bf16[1,128,4096]{2,1,0:T(8,128)(2,1)}, u32[]{:S(2)}) copy-start(bf16[1,128,4096]{2,1,0:T(8,128)(2,1)} %param.55) | copy-start | bytes 3145732
  7.2 86.8 %all-gather.3.cloned.1.call-start = ((), (), s32[]{:S(2)}) async-start(), calls=%async_computation.8 | async-start | bytes 9437184 | tf_op jit(solution)/shard_map/all_gather | solution.py:136
  9.7 12.4 %all-to-all-start.1 = ((bf16[128,8,128]{0,2,1:T(8,128)(2,1)}), bf16[128,8,128]{0,2,1:T(8,128)(2,1)S(1)}, u32[]{:S(2)}, u32[]{:S(2)}) async-start(bf16[128,8,128]{0,2,1:T(8,128)(2,1)} %bitcast.4), calls=%async_computation.1 | async-start | bytes 524288 | tf_op jit(solution)/shard_map/all_to_all | solution.py:129
  22.1 14.3 %all-to-all-start.2 = ((bf16[128,8,128]{0,2,1:T(8,128)(2,1)}), bf16[128,8,128]{0,2,1:T(8,128)(2,1)S(1)}, u32[]{:S(2)}, u32[]{:S(2)}) async-start(bf16[128,8,128]{0,2,1:T(8,128)(2,1)} %bitcast.8), calls=%async_computation.2 | async-start | bytes 524288 | tf_op jit(solution)/shard_map/all_to_all | solution.py:130
  26.5 14.2 %copy-start.69 = (s32[1,8]{1,0:T(1,128)S(1)}, s32[1,8]{1,0:T(1,128)}, u32[]{:S(2)}) copy-start(s32[1,8]{1,0:T(1,128)} %param.59) | copy-start | bytes 100
  36.4 31.1 %all-to-all-start = ((bf16[128,8,512]{0,2,1:T(8,128)(2,1)}), bf16[128,8,512]{0,2,1:T(8,128)(2,1)S(1)}, u32[]{:S(2)}, u32[]{:S(2)}) async-start(bf16[128,8,512]{0,2,1:T(8,128)(2,1)} %bitcast.1), calls=%async_computation | async-start | bytes 2097152 | tf_op jit(solution)/shard_map/all_to_all | solution.py:128
  40.7 153.0 %reduce-scatter.2.cloned.1.call-start = ((), (), s32[]{:S(2)}) async-start(), calls=%async_computation.7 | async-start | bytes 4456448 | tf_op jit(solution)/shard_map/reduce_scatter | solution.py:146
  41.0 35.8 %copy-start.15 = (bf16[8,128,128]{2,1,0:T(8,128)(2,1)}, bf16[8,128,128]{2,1,0:T(8,128)(2,1)S(1)}, u32[]{:S(2)}) copy-start(bf16[8,128,128]{2,1,0:T(8,128)(2,1)S(1)} %copy.71) | copy-start | bytes 786436
  41.5 41.1 %copy-start.40 = (bf16[4,128,128]{2,1,0:T(8,128)(2,1)}, bf16[4,128,128]{2,1,0:T(8,128)(2,1)S(1)}, u32[]{:S(2)}) copy-start(bf16[4,128,128]{2,1,0:T(8,128)(2,1)S(1)} %copy.68) | copy-start | bytes 393220
  68.8 1.5 copy-start.29
  70.2 8.5 %copy-start.58 = (f32[512]{0:T(512)}, f32[512]{0:T(512)S(1)}, u32[]{:S(2)}) copy-start(f32[512]{0:T(512)S(1)} %get-tuple-element.276) | copy-start | bytes 6148
  70.4 8.3 %copy-start.60 = (f32[512]{0:T(512)}, f32[512]{0:T(512)S(1)}, u32[]{:S(2)}) copy-start(f32[512]{0:T(512)S(1)} %fusion.73) | copy-start | bytes 6148
  70.7 9.8 %copy-start.25 = (f32[512,512]{0,1:T(8,128)}, f32[512,512]{0,1:T(8,128)S(1)}, u32[]{:S(2)}) copy-start(f32[512,512]{0,1:T(8,128)S(1)} %get-tuple-element.281) | copy-start | bytes 3145732
  71.3 11.1 %copy-start.23 = (f32[512,512]{0,1:T(8,128)}, f32[512,512]{0,1:T(8,128)S(1)}, u32[]{:S(2)}) copy-start(f32[512,512]{0,1:T(8,128)S(1)} %get-tuple-element.285) | copy-start | bytes 3145732
  71.9 11.7 %copy-start.27 = (f32[512,512]{0,1:T(8,128)}, f32[512,512]{0,1:T(8,128)S(1)}, u32[]{:S(2)}) copy-start(f32[512,512]{0,1:T(8,128)S(1)} %get-tuple-element.273) | copy-start | bytes 3145732
  71.9 11.7 %copy-start.62 = (f32[512]{0:T(512)}, f32[512]{0:T(512)S(1)}, u32[]{:S(2)}) copy-start(f32[512]{0:T(512)S(1)} %get-tuple-element.272) | copy-start | bytes 6148
  72.1 11.5 %copy-start.64 = (f32[512]{0:T(512)}, f32[512]{0:T(512)S(1)}, u32[]{:S(2)}) copy-start(f32[512]{0:T(512)S(1)} %fusion.71) | copy-start | bytes 6148
  91.0 1.9 copy-start
  94.0 9.3 %copy-start.34 = (bf16[512,512]{0,1:T(8,128)(2,1)S(1)}, bf16[512,512]{0,1:T(8,128)(2,1)}, u32[]{:S(2)}) copy-start(bf16[512,512]{0,1:T(8,128)(2,1)} %fusion.89) | copy-start | bytes 1572868
  94.0 9.3 %copy-start.41 = (bf16[4,128,128]{2,1,0:T(8,128)(2,1)S(1)}, bf16[4,128,128]{2,1,0:T(8,128)(2,1)}, u32[]{:S(2)}) copy-start(bf16[4,128,128]{2,1,0:T(8,128)(2,1)} %copy-done.40) | copy-start | bytes 393220
  94.0 9.3 %copy-start.51 = (bf16[512,128]{0,1:T(8,128)(2,1)S(1)}, bf16[512,128]{0,1:T(8,128)(2,1)}, u32[]{:S(2)}) copy-start(bf16[512,128]{0,1:T(8,128)(2,1)} %convolution_convert_fusion.7) | copy-start | bytes 393220
  94.0 9.3 %copy-start.52 = (bf16[512,128]{0,1:T(8,128)(2,1)S(1)}, bf16[512,128]{0,1:T(8,128)(2,1)}, u32[]{:S(2)}) copy-start(bf16[512,128]{0,1:T(8,128)(2,1)} %convolution_convert_fusion.6) | copy-start | bytes 393220
  94.0 9.3 %copy-start.53 = (bf16[512,128]{0,1:T(8,128)(2,1)S(1)}, bf16[512,128]{0,1:T(8,128)(2,1)}, u32[]{:S(2)}) copy-start(bf16[512,128]{0,1:T(8,128)(2,1)} %convolution_convert_fusion.5) | copy-start | bytes 393220
  94.0 9.3 %copy-start.54 = (bf16[512,128]{0,1:T(8,128)(2,1)S(1)}, bf16[512,128]{0,1:T(8,128)(2,1)}, u32[]{:S(2)}) copy-start(bf16[512,128]{0,1:T(8,128)(2,1)} %convolution_convert_fusion.4) | copy-start | bytes 393220
  94.0 9.3 %copy-start.55 = (bf16[512,128]{0,1:T(8,128)(2,1)S(1)}, bf16[512,128]{0,1:T(8,128)(2,1)}, u32[]{:S(2)}) copy-start(bf16[512,128]{0,1:T(8,128)(2,1)} %convolution_convert_fusion.2) | copy-start | bytes 393220
  94.0 9.3 %copy-start.56 = (bf16[512,128]{0,1:T(8,128)(2,1)S(1)}, bf16[512,128]{0,1:T(8,128)(2,1)}, u32[]{:S(2)}) copy-start(bf16[512,128]{0,1:T(8,128)(2,1)} %convolution_convert_fusion.1) | copy-start | bytes 393220
  94.0 9.3 %copy-start.57 = (bf16[512,128]{0,1:T(8,128)(2,1)S(1)}, bf16[512,128]{0,1:T(8,128)(2,1)}, u32[]{:S(2)}) copy-start(bf16[512,128]{0,1:T(8,128)(2,1)} %convolution_convert_fusion) | copy-start | bytes 393220
  94.0 16.0 %copy-start.70 = (bf16[1,1024,4096]{2,1,0:T(8,128)(2,1)S(1)}, bf16[1,1024,4096]{2,1,0:T(8,128)(2,1)}, u32[]{:S(2)}) copy-start(bf16[1,1024,4096]{2,1,0:T(8,128)(2,1)} %all-gather.3.cloned.1.call-done) | copy-start | bytes 25165828
  103.4 3.4 %copy-start.31 = (bf16[1024,512]{0,1:T(8,128)(2,1)}, bf16[1024,512]{0,1:T(8,128)(2,1)S(1)}, u32[]{:S(2)}) copy-start(bf16[1024,512]{0,1:T(8,128)(2,1)S(1)} %fusion.16) | copy-start | bytes 3145732
  104.5 1.8 copy-start.7
  116.2 3.1 %copy-start.26 = (f32[512,512]{0,1:T(8,128)S(1)}, f32[512,512]{0,1:T(8,128)}, u32[]{:S(2)}) copy-start(f32[512,512]{0,1:T(8,128)} %copy-done.25) | copy-start | bytes 3145732
  116.2 3.1 %copy-start.32 = (bf16[1024,512]{0,1:T(8,128)(2,1)S(1)}, bf16[1024,512]{0,1:T(8,128)(2,1)}, u32[]{:S(2)}) copy-start(bf16[1024,512]{0,1:T(8,128)(2,1)} %copy-done.31) | copy-start | bytes 3145732
  116.2 3.1 %copy-start.42 = (bf16[4,128,128]{2,1,0:T(8,128)(2,1)S(1)}, bf16[4,128,128]{2,1,0:T(8,128)(2,1)}, u32[]{:S(2)}) copy-start(bf16[4,128,128]{2,1,0:T(8,128)(2,1)} %copy-done.40) | copy-start | bytes 393220
  116.2 3.1 %copy-start.72 = (f32[512]{0:T(512)S(1)}, f32[512]{0:T(512)}, u32[]{:S(2)}) copy-start(f32[512]{0:T(512)} %get-tuple-element.264) | copy-start | bytes 6148
  119.3 1.8 copy-start.4
  119.3 1.8 copy-start.68
  119.6 2.5 %copy-start.38 = (bf16[512,512]{0,1:T(8,128)(2,1)}, bf16[512,512]{0,1:T(8,128)(2,1)S(1)}, u32[]{:S(2)}) copy-start(bf16[512,512]{0,1:T(8,128)(2,1)S(1)} %fusion.28) | copy-start | bytes 1572868
  119.6 1.9 copy-start.30
  121.6 1.9 copy-start.9
  121.6 1.6 copy-start.24
  121.6 1.6 copy-start.71
  123.2 1.8 copy-start.1
  123.2 1.8 copy-start.67
  123.5 2.5 %copy-start.39 = (bf16[512,512]{0,1:T(8,128)(2,1)}, bf16[512,512]{0,1:T(8,128)(2,1)S(1)}, u32[]{:S(2)}) copy-start(bf16[512,512]{0,1:T(8,128)(2,1)S(1)} %fusion.27) | copy-start | bytes 1572868
  128.1 21.4 %all-to-all-start.4 = ((bf16[8,128,128]{2,1,0:T(8,128)(2,1)}), bf16[8,128,128]{2,1,0:T(8,128)(2,1)}, u32[]{:S(2)}, u32[]{:S(2)}) async-start(bf16[8,128,128]{2,1,0:T(8,128)(2,1)} %bitcast.15), calls=%async_computation.4 | async-start | bytes 524288 | tf_op jit(solution)/shard_map/all_to_all | solution.py:155
  132.8 5.8 %copy-start.8 = (f32[512,1024]{1,0:T(8,128)S(1)}, f32[512,1024]{1,0:T(8,128)}, u32[]{:S(2)}) copy-start(f32[512,1024]{1,0:T(8,128)} %copy-done.6) | copy-start | bytes 6291460
  137.1 3.1 %copy-start.22 = (bf16[512,512]{0,1:T(8,128)(2,1)S(1)}, bf16[512,512]{0,1:T(8,128)(2,1)}, u32[]{:S(2)}) copy-start(bf16[512,512]{0,1:T(8,128)(2,1)} %copy-done.21) | copy-start | bytes 1572868
  137.1 3.1 %copy-start.33 = (bf16[1024,512]{0,1:T(8,128)(2,1)S(1)}, bf16[1024,512]{0,1:T(8,128)(2,1)}, u32[]{:S(2)}) copy-start(bf16[1024,512]{0,1:T(8,128)(2,1)} %copy-done.31) | copy-start | bytes 3145732
  138.6 1.9 copy-start.5
  140.5 1.7 copy-start.2
  141.2 1.4 copy-start.18
  142.7 1.9 copy-start.12
  142.7 3.0 %copy-start.10 = (bf16[512,1024]{1,0:T(8,128)(2,1)S(1)}, bf16[512,1024]{1,0:T(8,128)(2,1)}, u32[]{:S(2)}) copy-start(bf16[512,1024]{1,0:T(8,128)(2,1)} %copy-done.9) | copy-start | bytes 3145732
  146.8 2.3 %copy-start.37 = (bf16[512,512]{0,1:T(8,128)(2,1)S(1)}, bf16[512,512]{0,1:T(8,128)(2,1)}, u32[]{:S(2)}) copy-start(bf16[512,512]{0,1:T(8,128)(2,1)} %fusion.29) | copy-start | bytes 1572868
  147.9 6.4 %copy-start.36 = (bf16[512,512]{0,1:T(8,128)(2,1)S(1)}, bf16[512,512]{0,1:T(8,128)(2,1)}, u32[]{:S(2)}) copy-start(bf16[512,512]{0,1:T(8,128)(2,1)} %copy-done.35) | copy-start | bytes 1572868
  147.9 6.7 %copy-start.44 = (bf16[512,128]{1,0:T(8,128)(2,1)S(1)}, bf16[512,128]{1,0:T(8,128)(2,1)}, u32[]{:S(2)}) copy-start(bf16[512,128]{1,0:T(8,128)(2,1)} %fusion.49) | copy-start | bytes 393220
  147.9 6.7 %copy-start.45 = (bf16[512,128]{1,0:T(8,128)(2,1)S(1)}, bf16[512,128]{1,0:T(8,128)(2,1)}, u32[]{:S(2)}) copy-start(bf16[512,128]{1,0:T(8,128)(2,1)} %fusion.48) | copy-start | bytes 393220
  147.9 6.7 %copy-start.46 = (bf16[512,128]{1,0:T(8,128)(2,1)S(1)}, bf16[512,128]{1,0:T(8,128)(2,1)}, u32[]{:S(2)}) copy-start(bf16[512,128]{1,0:T(8,128)(2,1)} %fusion.53) | copy-start | bytes 393220
  147.9 6.7 %copy-start.47 = (bf16[512,128]{1,0:T(8,128)(2,1)S(1)}, bf16[512,128]{1,0:T(8,128)(2,1)}, u32[]{:S(2)}) copy-start(bf16[512,128]{1,0:T(8,128)(2,1)} %fusion.52) | copy-start | bytes 393220
  149.1 5.5 %copy-start.48 = (bf16[512,128]{1,0:T(8,128)(2,1)S(1)}, bf16[512,128]{1,0:T(8,128)(2,1)}, u32[]{:S(2)}) copy-start(bf16[512,128]{1,0:T(8,128)(2,1)} %fusion.51) | copy-start | bytes 393220
  149.1 5.6 %copy-start.49 = (bf16[512,128]{1,0:T(8,128)(2,1)S(1)}, bf16[512,128]{1,0:T(8,128)(2,1)}, u32[]{:S(2)}) copy-start(bf16[512,128]{1,0:T(8,128)(2,1)} %fusion.50) | copy-start | bytes 393220
  149.5 11.3 %all-to-all-start.5 = ((bf16[8,128,128]{2,1,0:T(8,128)(2,1)}), bf16[8,128,128]{2,1,0:T(8,128)(2,1)S(1)}, u32[]{:S(2)}, u32[]{:S(2)}) async-start(bf16[8,128,128]{2,1,0:T(8,128)(2,1)} %bitcast.17), calls=%async_computation.5 | async-start | bytes 524288 | tf_op jit(solution)/shard_map/all_to_all | solution.py:156
  160.7 19.5 %all-to-all-start.3 = ((bf16[8,128,512]{2,1,0:T(8,128)(2,1)}), bf16[8,128,512]{2,1,0:T(8,128)(2,1)S(1)}, u32[]{:S(2)}, u32[]{:S(2)}) async-start(bf16[8,128,512]{2,1,0:T(8,128)(2,1)} %bitcast.13), calls=%async_computation.3 | async-start | bytes 2097152 | tf_op jit(solution)/shard_map/all_to_all | solution.py:154
  (17 other events, 19.5 us)
Sparse Core Ops, SparseCore 0:
  9.7 67.3 all-gather.2
  116.3 77.3 reduce-scatter.1
where the time goes:
time: 205 us; the launch traced here: 202 us
  waiting for transfers between devices  69.6 us (34%)
  matrix products  58.1 us (28%)
  starting transfers between devices  28.7 us (14%)
  local copies, waits for them, and re-layouts  21.8 us (11%)
  between operations  15 us (7%)
  other arithmetic  9.16 us (4%)
    all_to_all x1, waiting for transfers between devices, body(): lax.all_to_all(queries[0], 'seq', split_axis=1, concat_axis=0, tiled=True)  26 us
    unnamed x149, local copies, waits for them, and re-layouts  15 us
    all_to_all x1, waiting for transfers between devices, body(): lax.all_to_all(grad_q, 'seq', split_axis=0, concat_axis=1, tiled=True)  12.1 us
    reduce_scatter x1, waiting for transfers between devices, body(): lax.psum_scatter(weight_acc.astype(jnp.bfloat16), 'dp', scatter_dimension...  11.6 us
    dot_general x8, matrix products, attend_back(): jnp.dot(grad_scores, key_all[:ending], preferred_element_type=jnp.float32)  9.36 us
    dot_general x1, matrix products, body(): lax.dot_general(piece, out_weight, (((1,), (1,)), ((), ())), preferred_el...  9.24 us
    dot_general x8, matrix products, attend(): jnp.dot(probs.astype(jnp.bfloat16), value_all[:ending], preferred_element...  8.69 us
    all_to_all x1, waiting for transfers between devices, body(): lax.all_to_all(values[0], 'seq', split_axis=1, concat_axis=0, tiled=True)  8.62 us
  transfers between devices with their start and end apart: 8, of which 6 were waited for; matrix products, arithmetic and copies ran while one was open for 28% of the time, Pallas kernels for 0%

commit v1 on v0

v1 whole, which is shorter than its diff:
```python
import math

import jax
import jax.numpy as jnp
from jax import lax
from jax.experimental import pallas as pl
from jax.experimental.pallas import tpu as pltpu
from jax.sharding import PartitionSpec as P

MESH = pl.DeviceIdType.MESH
F32 = jnp.float32
BF16 = jnp.bfloat16
T = 1024
R = 128
H = 4
DH = 128
F = H * DH
D = 4096
B = 256
NB = T // B
NC = 8
CW = D // NC
SCALE = 1.0 / math.sqrt(DH)
NT = (((1,), (1,)), ((), ()))


def dot(a, b):
    return jnp.dot(a, b, preferred_element_type=F32)


def dot_nt(a, b):
    return lax.dot_general(a, b, NT, preferred_element_type=F32)


def mult(x, n):
    return pl.multiple_of(x, n)


def kernel(
    go, q, k, v, w, starts,
    dq_o, dk_o, dv_o, wg_o,
    qs, ks, vs, kT, vT, G, ow, PT, OT, bias, dOacc, dO, Wb, rx, rz, s1b, s2b, rx2, rz2, fin,
    dQT, dqs, dKa, dVa, dkb, dvb,
    s_q, r_q, s_k, r_k, s_v, r_v, l_q, l_k, l_v,
    s_ag, r_m, r_p, r_o, r_s, l_g, l_w,
    s_x, r_x, s_z, r_z, s_x2, r_x2, s_z2, r_z2,
    s_dq, r_dq, s_dk, r_dk, s_dv, r_dv, l_dq, l_dk, l_dv,
):
    dp = lax.axis_index("dp")
    me = lax.axis_index("seq")
    X, Z = dp // 4, lax.rem(dp, 4)
    Y, C = me // 2, lax.rem(me, 2)
    par = lax.rem(Z, 2)

    def seq_dev(s):
        return (dp, s)

    def grid_dev(x, z):
        return (x * 4 + z, me)

    def remote(src, dst, ss, rs, dev):
        return pltpu.make_async_remote_copy(
            src_ref=src, dst_ref=dst, send_sem=ss, recv_sem=rs, device_id=dev, device_id_type=MESH
        )

    up = seq_dev(lax.rem(Y + 1, 4) * 2 + C)
    down = seq_dev(lax.rem(Y + 3, 4) * 2 + C)
    sib = seq_dev(Y * 2 + 1 - C)

    barrier = pltpu.get_barrier_semaphore()
    for o in range(1, 8):
        pl.semaphore_signal(
            barrier, 1, device_id=seq_dev(lax.rem(me + o, 8)), device_id_type=MESH
        )
    for o in range(1, 4):
        pl.semaphore_signal(
            barrier, 1, device_id=grid_dev(lax.rem(X + o, 4), Z), device_id_type=MESH
        )
        pl.semaphore_signal(
            barrier, 1, device_id=grid_dev(X, lax.rem(Z + o, 4)), device_id_type=MESH
        )
    pl.semaphore_wait(barrier, 13)

    my_rows = pl.ds(mult(me * R, R), R)

    for o in (4, 5, 3, 2, 6, 1, 7):
        g = lax.rem(me + o, 8)
        remote(k.at[:, pl.ds(mult(g * DH, DH), DH)], ks.at[my_rows], s_k, r_k, seq_dev(g)).start()
        remote(v.at[:, pl.ds(mult(g * DH, DH), DH)], vs.at[my_rows], s_v, r_v, seq_dev(g)).start()
        remote(q.at[:, pl.ds(mult(g * F, F), F)], qs.at[my_rows], s_q, r_q, seq_dev(g)).start()
    own_q = pltpu.make_async_copy(q.at[:, pl.ds(mult(me * F, F), F)], qs.at[my_rows], l_q)
    own_k = pltpu.make_async_copy(k.at[:, pl.ds(mult(me * DH, DH), DH)], ks.at[my_rows], l_k)
    own_v = pltpu.make_async_copy(v.at[:, pl.ds(mult(me * DH, DH), DH)], vs.at[my_rows], l_v)
    own_q.start()
    own_k.start()
    own_v.start()

    def chunk_cols(j):
        xb = lax.rem(X + 1 + j // 2, 4)
        zp = lax.rem(Z // 2 + 1 + lax.rem(j, 2), 2)
        return pl.ds(mult((xb * 2 + zp) * CW, CW), CW)

    def rows_of(s):
        return pl.ds(mult(s * R, R), R)

    def send_own(j):
        src = go.at[:, chunk_cols(j)]
        dst = G.at[j, my_rows]
        remote(src, dst, s_ag, r_p.at[j], up).start()
        remote(src, dst, s_ag, r_m.at[j], down).start()
        remote(src, dst, s_ag, r_s.at[j], sib).start()

    from_down = lax.rem(Y + 3, 4) * 2 + C
    from_up = lax.rem(Y + 1, 4) * 2 + C
    from_opp = lax.rem(Y + 2, 4) * 2 + C

    def piece(j, s):
        return G.at[j, rows_of(s)]

    def arrived(j, s, sem):
        pltpu.make_async_copy(piece(j, s), piece(j, s), sem).wait()

    def relay(j, upward):
        lo, hi = piece(j, from_down), piece(j, from_up)
        if upward:
            arrived(j, from_down, r_p.at[j])
            remote(lo, lo, s_ag, r_o.at[j], up).start()
            arrived(j, from_up, r_m.at[j])
        else:
            arrived(j, from_up, r_m.at[j])
            remote(hi, hi, s_ag, r_o.at[j], down).start()
            arrived(j, from_down, r_p.at[j])
        remote(lo, lo, s_ag, r_s.at[j], sib).start()
        remote(hi, hi, s_ag, r_s.at[j], sib).start()

    for j in range(NC):
        pltpu.make_async_copy(go.at[:, chunk_cols(j)], G.at[j, my_rows], l_g).start()
        pltpu.make_async_copy(w.at[:, chunk_cols(j)], ow.at[j], l_w).start()
    for j in range(4):
        send_own(j)

    for i in range(NB):
        t = i * B + lax.broadcasted_iota(jnp.int32, (1, B), 1)
        opening = jnp.zeros((1, B), jnp.int32)
        for d in range(8):
            s = starts[0, d]
            opening = jnp.maximum(opening, jnp.where(s <= t, s, 0))
        n = (i + 1) * B
        u = lax.broadcasted_iota(jnp.int32, (n, B), 0)
        bias[i, :n] = jnp.where((u >= opening) & (u <= t), 0.0, -1e30)

    own_q.wait()
    own_k.wait()
    own_v.wait()
    pltpu.make_async_copy(ks.at[pl.ds(0, 7 * R)], ks.at[pl.ds(0, 7 * R)], r_k).wait()
    pltpu.make_async_copy(vs.at[pl.ds(0, 7 * R)], vs.at[pl.ds(0, 7 * R)], r_v).wait()
    for i in range(NB):
        kT[i] = ks[pl.ds(i * B, B)].T
    vT[...] = vs[...].T
    pltpu.make_async_copy(qs.at[pl.ds(0, 7 * R)], qs.at[pl.ds(0, 7 * R)], r_q).wait()

    def forward(h, upward):
        cols = pl.ds(mult(h * DH, DH), DH)
        for i in range(NB):
            n = (i + 1) * B
            st = dot_nt(ks[:n], qs[pl.ds(i * B, B), cols])
            st = st * (SCALE * math.log2(math.e)) + bias[i, :n]
            top = jnp.max(st, axis=0, keepdims=True)
            p = jnp.exp2(st - top)
            p = (p * (1.0 / jnp.sum(p, axis=0, keepdims=True))).astype(BF16)
            PT[h, i, :n] = p
            OT[cols, pl.ds(i * B, B)] = dot(vT[:, :n], p).astype(BF16)
        relay(h, upward)
        send_own(h + 4)

    def forward_pair(g, _):
        forward(2 * g, True)
        forward(2 * g + 1, False)
        return 0

    lax.fori_loop(0, H // 2, forward_pair, 0)

    pltpu.make_async_copy(G.at[0], G.at[0], l_g).wait()
    pltpu.make_async_copy(ow, ow, l_w).wait()

    def gathered(j):
        arrived(j, from_opp, r_o.at[j])
        opp = piece(j, from_opp)
        remote(opp, opp, s_ag, r_s.at[j], sib).start()
        half = G.at[j, pl.ds(0, 4 * R)]
        pltpu.make_async_copy(half, half, r_s.at[j]).wait()

    def dense(j):
        part = dot_nt(G[j], ow[j])

        @pl.when(j == 0)
        def _():
            dOacc[...] = part

        @pl.when(j > 0)
        def _():
            dOacc[...] += part

        Wb[j] = dot(OT[...], G[j]).astype(BF16)

    def chunk_pair(g, _):
        other = 1 - Z // 2
        for e in range(2):
            j = 2 * g + e
            gathered(j)
            dense(j)

            @pl.when(g < 2)
            def _():
                relay(j + 4, e == 0)

            @pl.when(g < 3)
            def _():
                remote(
                    Wb.at[j, pl.ds(0, 256)], rx.at[g, e], s_x, r_x,
                    grid_dev(lax.rem(X + 1 + g, 4), Z),
                ).start()

            if e == 0:
                for c in range(2):
                    zz = 2 * other + c
                    slot = lax.rem(zz - Z + 4, 4) - 1
                    remote(
                        Wb.at[j, pl.ds(256, 256), pl.ds(c * 256, 256)], rz.at[slot, g], s_z, r_z,
                        grid_dev(X, zz),
                    ).start()
            else:
                zz = Z + 1 - 2 * par
                slot = lax.rem(zz - Z + 4, 4) - 1
                remote(
                    Wb.at[j, pl.ds(256, 256), pl.ds(mult((1 - par) * 256, 256), 256)],
                    rz.at[slot, g], s_z, r_z, grid_dev(X, zz),
                ).start()
        return 0

    lax.fori_loop(0, NC // 2, chunk_pair, 0)
    dO[...] = dOacc[...].astype(BF16)
    dKa[...] = jnp.zeros_like(dKa)
    dVa[...] = jnp.zeros_like(dVa)

    def backward(b):
        rows = pl.ds(mult(b * B, B), B)
        hc = [pl.ds(h * DH, DH) for h in range(H)]
        deltas = []
        for h in range(H):
            gT = dO[rows, hc[h]].astype(F32).T
            deltas.append(jnp.sum(gT * OT[hc[h], rows].astype(F32), axis=0, keepdims=True))
        dQT[...] = jnp.zeros_like(dQT)

        def block(kb, _):
            keys = pl.ds(mult(kb * B, B), B)
            kk, vv = kT[kb], vs[keys]
            dk = jnp.zeros((B, DH), F32)
            dv = jnp.zeros((B, DH), F32)
            for h in range(H):
                p = PT[h, b, keys]
                g = dO[rows, hc[h]]
                dp_ = dot_nt(vv, g)
                ds = (p.astype(F32) * (dp_ - deltas[h])).astype(BF16)
                dv += dot(p, g)
                dk += dot(ds, qs[rows, hc[h]])
                dQT[h] += dot(kk, ds)
            dKa[keys] += dk
            dVa[keys] += dv
            return 0

        lax.fori_loop(0, b + 1, block, 0)
        for h in range(H):
            dqs[b, :, hc[h]] = (dQT[h].T * SCALE).astype(BF16)

    my_f = pl.ds(mult(me * F, F), F)
    my_d = pl.ds(mult(me * DH, DH), DH)

    def far_block(step, _):
        b = lax.rem(Y + 1 + step, 4)
        backward(b)
        for c in range(2):
            remote(
                dqs.at[b, pl.ds(c * R, R)], dq_o.at[:, my_f], s_dq, r_dq, seq_dev(b * 2 + c)
            ).start()
        return 0

    lax.fori_loop(0, 3, far_block, 0)
    backward(Y)
    other_rows = pl.ds(mult((1 - C) * R, R), R)
    own_rows = pl.ds(mult(C * R, R), R)
    remote(dqs.at[Y, other_rows], dq_o.at[:, my_f], s_dq, r_dq, sib).start()
    own_dq = pltpu.make_async_copy(dqs.at[Y, own_rows], dq_o.at[:, my_f], l_dq)
    own_dq.start()

    dkb[...] = (dKa[...] * SCALE).astype(BF16)
    dvb[...] = dVa[...].astype(BF16)
    for o in (4, 5, 3, 2, 6, 1, 7):
        g = lax.rem(me + o, 8)
        remote(dkb.at[rows_of(g)], dk_o.at[:, my_d], s_dk, r_dk, seq_dev(g)).start()
        remote(dvb.at[rows_of(g)], dv_o.at[:, my_d], s_dv, r_dv, seq_dev(g)).start()
    own_dk = pltpu.make_async_copy(dkb.at[my_rows], dk_o.at[:, my_d], l_dk)
    own_dv = pltpu.make_async_copy(dvb.at[my_rows], dv_o.at[:, my_d], l_dv)
    own_dk.start()
    own_dv.start()

    pltpu.make_async_copy(rx, rx, r_x).wait()
    for e in range(2):
        s = Wb[6 + e, :256].astype(F32)
        for i in range(3):
            s += rx[i, e].astype(F32)
        s1b[e] = s.astype(BF16)
    other = 1 - Z // 2
    for c in range(2):
        zz = 2 * other + c
        slot = lax.rem(zz - Z + 4, 4) - 1
        remote(
            s1b.at[0, :, pl.ds(c * 256, 256)], rx2.at[slot], s_x2, r_x2, grid_dev(X, zz)
        ).start()
    zz = Z + 1 - 2 * par
    slot = lax.rem(zz - Z + 4, 4) - 1
    remote(
        s1b.at[1, :, pl.ds(mult((1 - par) * 256, 256), 256)], rx2.at[slot], s_x2, r_x2,
        grid_dev(X, zz),
    ).start()

    pltpu.make_async_copy(rz, rz, r_z).wait()
    own_cols = pl.ds(mult(par * 256, 256), 256)
    for g in range(4):
        s = Wb[2 * g + 1, 256:, own_cols].astype(F32)
        for i in range(3):
            s += rz[i, g].astype(F32)
        if g < 3:
            s2b[g] = s.astype(BF16)
            remote(
                s2b.at[g], rz2.at[g], s_z2, r_z2, grid_dev(lax.rem(X + 1 + g, 4), Z)
            ).start()
        else:
            fin[...] = s

    pltpu.make_async_copy(rx2, rx2, r_x2).wait()
    norm = 1.0 / math.sqrt(T * 16)
    s = s1b[1, :, own_cols].astype(F32)
    for i in range(3):
        s += rx2[i].astype(F32)
    wg_o[:256] = s * norm
    pltpu.make_async_copy(rz2, rz2, r_z2).wait()
    s = fin[...]
    for i in range(3):
        s += rz2[i].astype(F32)
    wg_o[256:] = s * norm

    def drain(ref, *sems):
        for sem in sems:
            pltpu.make_async_copy(ref, ref, sem).wait()

    own_dq.wait()
    own_dk.wait()
    own_dv.wait()
    drain(qs.at[pl.ds(0, 7 * R)], s_q, s_dq, r_dq)
    drain(ks.at[pl.ds(0, 7 * R)], s_k, s_v, s_dk, s_dv, r_dk, r_dv)
    drain(G.at[pl.ds(0, 7)], s_ag)
    drain(rx, s_x)
    drain(rz, s_z)
    drain(rx2, s_x2, s_z2)


def body(grad_out, queries, keys, values, out_weight, doc_starts):
    vm = pltpu.VMEM
    dma = pltpu.SemaphoreType.DMA
    hbm = pl.BlockSpec(memory_space=pl.ANY)
    scratch = [
        vm((T, F), BF16),
        vm((T, DH), BF16),
        vm((T, DH), BF16),
        vm((NB, DH, B), BF16),
        vm((DH, T), BF16),
        vm((NC, T, CW), BF16),
        vm((NC, F, CW), BF16),
        vm((H, NB, T, B), BF16),
        vm((F, T), BF16),
        vm((NB, T, B), F32),
        vm((T, F), F32),
        vm((T, F), BF16),
        vm((NC, F, CW), BF16),
        vm((3, 2, 256, 512), BF16),
        vm((3, 4, 256, 256), BF16),
        vm((2, 256, 512), BF16),
        vm((3, 256, 256), BF16),
        vm((3, 256, 256), BF16),
        vm((3, 256, 256), BF16),
        vm((256, 256), F32),
        vm((H, DH, B), F32),
        vm((NB, B, F), BF16),
        vm((T, DH), F32),
        vm((T, DH), F32),
        vm((T, DH), BF16),
        vm((T, DH), BF16),
    ]
    scratch += [dma] * 9
    scratch += [dma, dma((NC,)), dma((NC,)), dma((NC,)), dma((NC,)), dma, dma]
    scratch += [dma] * 8
    scratch += [dma] * 9
    out = pl.pallas_call(
        kernel,
        name="attention_back",
        out_shape=(
            jax.ShapeDtypeStruct((R, D), BF16),
            jax.ShapeDtypeStruct((R, 1024), BF16),
            jax.ShapeDtypeStruct((R, 1024), BF16),
            jax.ShapeDtypeStruct((F, 256), F32),
        ),
        in_specs=[hbm] * 5 + [pl.BlockSpec(memory_space=pltpu.SMEM)],
        out_specs=(hbm, hbm, hbm, pl.BlockSpec(memory_space=pltpu.VMEM)),
        scratch_shapes=scratch,
        compiler_params=pltpu.CompilerParams(
            collective_id=0, has_side_effects=True, vmem_limit_bytes=60 * 1024 * 1024
        ),
    )(grad_out[0], queries[0], keys[0], values[0], out_weight, doc_starts)
    return (out[0][None], out[1][None], out[2][None], out[3])


def solution(mesh):
    return jax.shard_map(
        body,
        mesh=mesh,
        in_specs=(
            P("dp", "seq", None),
            P("dp", "seq", None),
            P("dp", "seq", None),
            P("dp", "seq", None),
            P("seq", None),
            P("dp", None),
        ),
        out_specs=(
            P("dp", "seq", None),
            P("dp", "seq", None),
            P("dp", "seq", None),
            P("seq", "dp"),
        ),
        check_vma=False,
    )
```

time: 205 us -> 104 us (0.51)
  Pallas kernels: 0 us -> 95.2 us
  waiting for transfers between devices: 69.6 us -> 0 us
  matrix products: 58.1 us -> 0 us
  starting transfers between devices: 28.7 us -> 0 us
  between operations: 15 us -> 0.64 us
  local copies, waits for them, and re-layouts: 21.8 us -> 7.49 us
  other arithmetic: 9.16 us -> 0 us
    pallas_call x0 -> x1, Pallas kernels: none -> 95.2 us  [body(): pl.pallas_call(kernel, name='attention_back', out_shape=(jax.ShapeDtypeSt...]
    dot_general x50 -> x0, matrix products: 58.1 us -> none  [the longest x8 9.36 us: attend_back(): jnp.dot(grad_scores, key_all[:ending], preferred_element_type=jnp.float32)]
    all_to_all x6 -> x0, waiting for transfers between devices: 57.2 us -> none  [the longest x1 26 us: body(): lax.all_to_all(queries[0], 'seq', split_axis=1, concat_axis=0, tiled=True)]
    all_to_all x6 -> x0, starting transfers between devices: 28.7 us -> none  [the longest x1 5.96 us: body(): lax.all_to_all(keys[0], 'seq', split_axis=1, concat_axis=0, tiled=True)]
    reduce_scatter x1 -> x0, waiting for transfers between devices: 11.6 us -> none  [body(): lax.psum_scatter(weight_acc.astype(jnp.bfloat16), 'dp', scatter_dimension...]
    unnamed x149 -> x4, local copies, waits for them, and re-layouts: 15 us -> 7.49 us
    all_to_all x6 -> x0, local copies, waits for them, and re-layouts: 3.54 us -> none  [the longest x1 1.3 us: body(): lax.all_to_all(queries[0], 'seq', split_axis=1, concat_axis=0, tiled=True)]
    broadcast_in_dim x3 -> x0, local copies, waits for them, and re-layouts: 2.94 us -> none  [body(): return (back_q[None], back_k[None], back_v[None], weight_grad)]
  transfers between devices with their start and end apart: 8 -> 0, of which waited for: 6 -> 0; matrix products, arithmetic and copies ran while one was open for 28% -> 0% of each run, Pallas kernels for 0% -> 0%
where the time goes in v1:
time: 104 us; the launch traced here: 103 us
  Pallas kernels  95.2 us (92%)
  local copies, waits for them, and re-layouts  7.49 us (7%)
    pallas_call x1, Pallas kernels, body(): pl.pallas_call(kernel, name='attention_back', out_shape=(jax.ShapeDtypeSt...  95.2 us
    unnamed x4, local copies, waits for them, and re-layouts  7.49 us

profile of v1, /device:TPU:1, one launch (start us, length us, event | category | flops | bytes accessed | tf_op | source)
XLA Modules:
  0.0 103.3 jit_solution(6311150986904353129)
XLA Ops:
  0.6 95.2 %attention_back.1 = (bf16[128,4096]{1,0:T(8,128)(2,1)}, bf16[128,1024]{1,0:T(8,128)(2,1)}, bf16[128,1024]{1,0:T(8,128)(2,1)}, f32[512,256]{1,0:T(8,128)}) custom-call(bf16[128,4096]{1,0:T(8,128)(2,1)} %bitcast.8, bf16[128,4096]{1,0:T(8,128)(2,1)} %bitcast.9, bf16[128,1024]{1,0:T(8,128)(2,1)} %bitcast.10, bf16[128,1024]{1,0:T(8,128)(2,1)} %bitcast.11, ...), custom_call_target="tpu_custom_call" | custom-call | tf_op jit(solution)/shard_map/attention_back/pallas_call | solution.py:404
  95.8 2.3 %copy.14 = bf16[1,128,4096]{2,1,0:T(8,128)(2,1)} copy(bf16[1,128,4096]{2,1,0:T(8,128)(2,1)} %bitcast.7) | data formatting | bytes 2097152
  98.1 1.7 %copy.15 = bf16[1,128,1024]{2,1,0:T(8,128)(2,1)} copy(bf16[1,128,1024]{2,1,0:T(8,128)(2,1)} %bitcast.13) | data formatting | bytes 524288
  99.8 1.7 %copy.16 = bf16[1,128,1024]{2,1,0:T(8,128)(2,1)} copy(bf16[1,128,1024]{2,1,0:T(8,128)(2,1)} %bitcast.12) | data formatting | bytes 524288
  101.4 1.9 %copy.17 = f32[512,256]{1,0:T(8,128)} copy(f32[512,256]{1,0:T(8,128)} %get-tuple-element.19) | data formatting | bytes 1048576

commit v2 on v1

v2 whole, which is shorter than its diff:
```python
import math

import jax
import jax.numpy as jnp
from jax import lax
from jax.experimental import pallas as pl
from jax.experimental.pallas import tpu as pltpu
from jax.sharding import PartitionSpec as P

MESH = pl.DeviceIdType.MESH
F32 = jnp.float32
BF16 = jnp.bfloat16
T = 1024
R = 128
H = 4
DH = 128
F = H * DH
D = 4096
B = 256
NB = T // B
NC = 8
CW = D // NC
CHUNK_X = (2, 2, 1, 3, 1, 3, 0, 0)
EARLY = 2
CHUNK_OWN = (0, 1, 0, 0, 1, 1, 0, 1)
SCALE = 1.0 / math.sqrt(DH)
NT = (((1,), (1,)), ((), ()))


def dot(a, b):
    return jnp.dot(a, b, preferred_element_type=F32)


def dot_nt(a, b):
    return lax.dot_general(a, b, NT, preferred_element_type=F32)


def mult(x, n):
    return pl.multiple_of(x, n)


def kernel(
    go, q, k, v, w, starts,
    dq_o, dk_o, dv_o, wg_o,
    qs, ks, vs, kT, vT, G, ow, PT, OT, bias, dOacc, dO, Wacc, Wb, rx, rz, s1b, s2b, rx2, rz2, fin,
    dqs, dKa, dVa, dkb, dvb,
    s_q, r_q, s_k, r_k, s_v, r_v, l_q, l_k, l_v,
    s_ag, r_m, r_p, r_o, r_own, r_near, r_opp, l_g, l_w,
    s_x, r_x, s_z, s_x2, r_x2, s_z2, r_z2, r_z,
    s_dq, r_dq, s_dk, r_dk, s_dv, r_dv, l_dq, l_dk, l_dv,
):
    dp = lax.axis_index("dp")
    me = lax.axis_index("seq")
    X, Z = dp // 4, lax.rem(dp, 4)
    Y, C = me // 2, lax.rem(me, 2)
    par = lax.rem(Z, 2)

    def seq_dev(s):
        return (dp, s)

    def grid_dev(x, z):
        return (x * 4 + z, me)

    def remote(src, dst, ss, rs, dev):
        return pltpu.make_async_remote_copy(
            src_ref=src, dst_ref=dst, send_sem=ss, recv_sem=rs, device_id=dev, device_id_type=MESH
        )

    up = seq_dev(lax.rem(Y + 1, 4) * 2 + C)
    down = seq_dev(lax.rem(Y + 3, 4) * 2 + C)
    sib = seq_dev(Y * 2 + 1 - C)

    barrier = pltpu.get_barrier_semaphore()
    for o in range(1, 8):
        pl.semaphore_signal(
            barrier, 1, device_id=seq_dev(lax.rem(me + o, 8)), device_id_type=MESH
        )
    for o in range(1, 4):
        pl.semaphore_signal(
            barrier, 1, device_id=grid_dev(lax.rem(X + o, 4), Z), device_id_type=MESH
        )
        pl.semaphore_signal(
            barrier, 1, device_id=grid_dev(X, lax.rem(Z + o, 4)), device_id_type=MESH
        )
    pl.semaphore_wait(barrier, 13)

    my_rows = pl.ds(mult(me * R, R), R)

    for o in (4, 5, 3, 2, 6, 1, 7):
        g = lax.rem(me + o, 8)
        remote(k.at[:, pl.ds(mult(g * DH, DH), DH)], ks.at[my_rows], s_k, r_k, seq_dev(g)).start()
        remote(v.at[:, pl.ds(mult(g * DH, DH), DH)], vs.at[my_rows], s_v, r_v, seq_dev(g)).start()
        remote(q.at[:, pl.ds(mult(g * F, F), F)], qs.at[my_rows], s_q, r_q, seq_dev(g)).start()
    own_q = pltpu.make_async_copy(q.at[:, pl.ds(mult(me * F, F), F)], qs.at[my_rows], l_q)
    own_k = pltpu.make_async_copy(k.at[:, pl.ds(mult(me * DH, DH), DH)], ks.at[my_rows], l_k)
    own_v = pltpu.make_async_copy(v.at[:, pl.ds(mult(me * DH, DH), DH)], vs.at[my_rows], l_v)
    own_q.start()
    own_k.start()
    own_v.start()

    def chunk_cols(j):
        xb = lax.rem(X + CHUNK_X[j], 4)
        zp = Z // 2 if CHUNK_OWN[j] else 1 - Z // 2
        return pl.ds(mult((xb * 2 + zp) * CW, CW), CW)

    def rows_of(s):
        return pl.ds(mult(s * R, R), R)

    def block_of(b):
        return pl.ds(mult(b * B, B), B)

    def send_own(j):
        src = go.at[:, chunk_cols(j)]
        dst = G.at[j, my_rows]
        remote(src, dst, s_ag, r_p.at[j], up).start()
        remote(src, dst, s_ag, r_m.at[j], down).start()

    y_up, y_down, y_opp = lax.rem(Y + 1, 4), lax.rem(Y + 3, 4), lax.rem(Y + 2, 4)
    from_down, from_up, from_opp = y_down * 2 + C, y_up * 2 + C, y_opp * 2 + C

    def piece(j, s):
        return G.at[j, rows_of(s)]

    def arrived(j, s, sem):
        pltpu.make_async_copy(piece(j, s), piece(j, s), sem).wait()

    def relay(j):
        lo, hi = piece(j, from_down), piece(j, from_up)
        if j % 2 == 0:
            arrived(j, from_down, r_p.at[j])
            remote(lo, lo, s_ag, r_o.at[j], up).start()
            arrived(j, from_up, r_m.at[j])
        else:
            arrived(j, from_up, r_m.at[j])
            remote(hi, hi, s_ag, r_o.at[j], down).start()
            arrived(j, from_down, r_p.at[j])
        remote(lo, lo, s_ag, r_near.at[j], sib).start()
        remote(hi, hi, s_ag, r_near.at[j], sib).start()

    for j in range(NC):
        pltpu.make_async_copy(go.at[:, chunk_cols(j)], G.at[j, my_rows], l_g).start()
        pltpu.make_async_copy(w.at[:, chunk_cols(j)], ow.at[j], l_w).start()
    for j in range(4):
        send_own(j)
    for j in range(NC):
        remote(go.at[:, chunk_cols(j)], G.at[j, my_rows], s_ag, r_own.at[j], sib).start()

    for i in range(NB):
        t = i * B + lax.broadcasted_iota(jnp.int32, (1, B), 1)
        opening = jnp.zeros((1, B), jnp.int32)
        for d in range(8):
            s = starts[0, d]
            opening = jnp.maximum(opening, jnp.where(s <= t, s, 0))
        n = (i + 1) * B
        u = lax.broadcasted_iota(jnp.int32, (n, B), 0)
        bias[i, :n] = jnp.where((u >= opening) & (u <= t), 0.0, -1e30)
    dKa[...] = jnp.zeros_like(dKa)
    dVa[...] = jnp.zeros_like(dVa)

    pltpu.make_async_copy(G.at[0], G.at[0], l_g).wait()
    pltpu.make_async_copy(ow, ow, l_w).wait()

    def project(j, b, first):
        rows = block_of(b)
        part = dot_nt(G[j, rows], ow[j])
        dOacc[rows] = part if first else dOacc[rows] + part

    def projected(b):
        rows = block_of(b)
        dO[rows] = dOacc[rows].astype(BF16)

    for j in range(NC):
        arrived(j, me + 1 - 2 * C, r_own.at[j])
        project(j, Y, j == 0)
    projected(Y)

    own_q.wait()
    own_k.wait()
    own_v.wait()
    pltpu.make_async_copy(ks.at[pl.ds(0, 7 * R)], ks.at[pl.ds(0, 7 * R)], r_k).wait()
    pltpu.make_async_copy(vs.at[pl.ds(0, 7 * R)], vs.at[pl.ds(0, 7 * R)], r_v).wait()
    kT[...] = ks[...].T
    vT[...] = vs[...].T
    pltpu.make_async_copy(qs.at[pl.ds(0, 7 * R)], qs.at[pl.ds(0, 7 * R)], r_q).wait()

    for h in range(H):
        cols = pl.ds(h * DH, DH)
        for i in range(NB):
            n = (i + 1) * B
            st = dot_nt(ks[:n], qs[pl.ds(i * B, B), cols])
            st = st * (SCALE * math.log2(math.e)) + bias[i, :n]
            top = jnp.max(st, axis=0, keepdims=True)
            p = jnp.exp2(st - top)
            p = (p * (1.0 / jnp.sum(p, axis=0, keepdims=True))).astype(BF16)
            PT[h, i, :n] = p
            OT[cols, pl.ds(i * B, B)] = dot(vT[:, :n], p).astype(BF16)
        if h < EARLY:
            relay(h)
        send_own(h + 4)

    hc = [pl.ds(h * DH, DH) for h in range(H)]

    def backward(b):
        rows = block_of(b)

        def pair(n, g):
            cols = [pl.ds(mult((2 * g + e) * DH, DH), DH) for e in range(2)]
            ps, gs, dss = [], [], []
            for e in range(2):
                grad = dO[rows, cols[e]]
                gT = grad.astype(F32).T
                delta = jnp.sum(gT * OT[cols[e], rows].astype(F32), axis=0, keepdims=True)
                p = PT[2 * g + e, b, :n]
                ds = (p.astype(F32) * (dot_nt(vs[:n], grad) - delta)).astype(BF16)
                dqs[b, :, cols[e]] = (dot(kT[:, :n], ds).T * SCALE).astype(BF16)
                ps.append(p)
                gs.append(grad)
                dss.append(ds)
            dVa[:n] += dot(jnp.concatenate(ps, axis=1), jnp.concatenate(gs, axis=0))
            qq = jnp.concatenate([qs[rows, c] for c in cols], axis=0)
            dKa[:n] += dot(jnp.concatenate(dss, axis=1), qq)

        for i in range(NB):

            @pl.when(b == i)
            def _():
                @pl.loop(0, H // 2)
                def _(g):
                    pair((i + 1) * B, g)

    my_f = pl.ds(mult(me * F, F), F)
    my_d = pl.ds(mult(me * DH, DH), DH)

    def send_dq(b):
        for c in range(2):
            remote(
                dqs.at[b, pl.ds(c * R, R)], dq_o.at[:, my_f], s_dq, r_dq, seq_dev(b * 2 + c)
            ).start()

    backward(Y)
    other_rows = pl.ds(mult((1 - C) * R, R), R)
    own_rows = pl.ds(mult(C * R, R), R)
    remote(dqs.at[Y, other_rows], dq_o.at[:, my_f], s_dq, r_dq, sib).start()
    own_dq = pltpu.make_async_copy(dqs.at[Y, own_rows], dq_o.at[:, my_f], l_dq)
    own_dq.start()

    def opposite(j):
        arrived(j, from_opp, r_o.at[j])
        opp = piece(j, from_opp)
        remote(opp, opp, s_ag, r_opp.at[j], sib).start()

    def near_here(j):
        half = G.at[j, pl.ds(0, 2 * R)]
        pltpu.make_async_copy(half, half, r_near.at[j]).wait()

    other = 1 - Z // 2

    def z_slot(zz):
        return lax.rem(zz - Z + 4, 4) - 1

    def scatter(j):
        dx = CHUNK_X[j]
        if dx:
            remote(
                Wb.at[j, pl.ds(0, 256)], rx.at[dx - 1, CHUNK_OWN[j]], s_x, r_x,
                grid_dev(lax.rem(X + dx, 4), Z),
            ).start()
        if CHUNK_OWN[j]:
            sends = [(mult((1 - par) * 256, 256), Z + 1 - 2 * par)]
        else:
            sends = [(c * 256, 2 * other + c) for c in range(2)]
        for col, zz in sends:
            remote(
                Wb.at[j, pl.ds(256, 256), pl.ds(col, 256)], rz.at[dx, z_slot(zz)], s_z, r_z.at[dx],
                grid_dev(X, zz),
            ).start()

    def near(j):
        near_here(j)
        s = None
        for b in (Y, y_up, y_down):
            d = dot(OT[:, block_of(b)], G[j, block_of(b)])
            s = d if s is None else s + d
        Wacc[j - 2] = s
        for b in (y_up, y_down):
            project(j, b, False)

    def full(j):
        arrived(j, y_opp * 2 + 1 - C, r_opp.at[j])
        near_here(j)
        for b in (y_up, y_down, y_opp):
            project(j, b, j == 0)
        Wb[j] = dot(OT[...], G[j]).astype(BF16)
        scatter(j)

    def finish(j):
        arrived(j, y_opp * 2 + 1 - C, r_opp.at[j])
        project(j, y_opp, False)
        Wb[j] = (Wacc[j - 2] + dot(OT[:, block_of(y_opp)], G[j, block_of(y_opp)])).astype(BF16)
        scatter(j)

    relay(2)
    relay(3)
    opposite(0)
    full(0)
    opposite(1)
    relay(4)
    near(2)
    full(1)
    relay(5)
    near(3)
    near(4)
    relay(6)
    near(5)
    relay(7)
    near(6)
    near(7)
    projected(y_up)
    projected(y_down)
    opposite(2)
    opposite(3)
    backward(y_up)
    send_dq(y_up)
    finish(2)
    finish(3)
    opposite(4)
    opposite(5)
    backward(y_down)
    send_dq(y_down)
    opposite(6)
    opposite(7)
    for j in range(4, NC):
        finish(j)
    projected(y_opp)
    backward(y_opp)
    send_dq(y_opp)

    dkb[...] = (dKa[...] * SCALE).astype(BF16)
    dvb[...] = dVa[...].astype(BF16)
    for o in (4, 5, 3, 2, 6, 1, 7):
        g = lax.rem(me + o, 8)
        remote(dkb.at[rows_of(g)], dk_o.at[:, my_d], s_dk, r_dk, seq_dev(g)).start()
        remote(dvb.at[rows_of(g)], dv_o.at[:, my_d], s_dv, r_dv, seq_dev(g)).start()
    own_dk = pltpu.make_async_copy(dkb.at[my_rows], dk_o.at[:, my_d], l_dk)
    own_dv = pltpu.make_async_copy(dvb.at[my_rows], dv_o.at[:, my_d], l_dv)
    own_dk.start()
    own_dv.start()

    chunk_at = {(CHUNK_X[j], CHUNK_OWN[j]): j for j in range(NC)}
    own_cols = pl.ds(mult(par * 256, 256), 256)

    def z_sum(dx):
        pltpu.make_async_copy(rz.at[dx], rz.at[dx], r_z.at[dx]).wait()
        s = Wb[chunk_at[dx, 1], 256:, own_cols].astype(F32)
        for i in range(3):
            s += rz[dx, i].astype(F32)
        if dx:
            s2b[dx - 1] = s.astype(BF16)
            remote(
                s2b.at[dx - 1], rz2.at[dx - 1], s_z2, r_z2, grid_dev(lax.rem(X + dx, 4), Z)
            ).start()
        else:
            fin[...] = s

    z_sum(2)
    z_sum(1)
    z_sum(3)
    pltpu.make_async_copy(rx, rx, r_x).wait()
    for e in range(2):
        s = Wb[chunk_at[0, e], :256].astype(F32)
        for i in range(3):
            s += rx[i, e].astype(F32)
        s1b[e] = s.astype(BF16)
    x_sends = [(0, c * 256, 2 * other + c) for c in range(2)]
    x_sends.append((1, mult((1 - par) * 256, 256), Z + 1 - 2 * par))
    for e, col, zz in x_sends:
        remote(
            s1b.at[e, :, pl.ds(col, 256)], rx2.at[z_slot(zz)], s_x2, r_x2, grid_dev(X, zz)
        ).start()

    z_sum(0)
    pltpu.make_async_copy(rx2, rx2, r_x2).wait()
    norm = 1.0 / math.sqrt(T * 16)
    s = s1b[1, :, own_cols].astype(F32)
    for i in range(3):
        s += rx2[i].astype(F32)
    wg_o[:256] = s * norm
    pltpu.make_async_copy(rz2, rz2, r_z2).wait()
    s = fin[...]
    for i in range(3):
        s += rz2[i].astype(F32)
    wg_o[256:] = s * norm

    def drain(ref, *sems):
        for sem in sems:
            pltpu.make_async_copy(ref, ref, sem).wait()

    own_dq.wait()
    own_dk.wait()
    own_dv.wait()
    drain(qs.at[pl.ds(0, 7 * R)], s_q, s_dq, r_dq)
    drain(ks.at[pl.ds(0, 7 * R)], s_k, s_v, s_dk, s_dv, r_dk, r_dv)
    drain(G.at[pl.ds(0, 7)], s_ag)
    drain(rx, s_x)
    drain(rz, s_z)
    drain(rx2, s_x2, s_z2)


def write_out(a, b, c, d, ao, bo, co, do, sem):
    copies = [
        pltpu.make_async_copy(src, dst, sem.at[i])
        for i, (src, dst) in enumerate(((a, ao), (b, bo), (c, co), (d, do)))
    ]
    for copy in copies:
        copy.start()
    for copy in copies:
        copy.wait()


def body(grad_out, queries, keys, values, out_weight, doc_starts):
    vm = pltpu.VMEM
    dma = pltpu.SemaphoreType.DMA
    hbm = pl.BlockSpec(memory_space=pl.ANY)
    scratch = [
        vm((T, F), BF16),
        vm((T, DH), BF16),
        vm((T, DH), BF16),
        vm((DH, T), BF16),
        vm((DH, T), BF16),
        vm((NC, T, CW), BF16),
        vm((NC, F, CW), BF16),
        vm((H, NB, T, B), BF16),
        vm((F, T), BF16),
        vm((NB, T, B), F32),
        vm((T, F), F32),
        vm((T, F), BF16),
        vm((NC - 2, F, CW), F32),
        vm((NC, F, CW), BF16),
        vm((3, 2, 256, 512), BF16),
        vm((4, 3, 256, 256), BF16),
        vm((2, 256, 512), BF16),
        vm((3, 256, 256), BF16),
        vm((3, 256, 256), BF16),
        vm((3, 256, 256), BF16),
        vm((256, 256), F32),
        vm((NB, B, F), BF16),
        vm((T, DH), F32),
        vm((T, DH), F32),
        vm((T, DH), BF16),
        vm((T, DH), BF16),
    ]
    scratch += [dma] * 9
    scratch += [dma] + [dma((NC,))] * 6 + [dma] * 2
    scratch += [dma] * 7 + [dma((4,))]
    scratch += [dma] * 9
    shapes = (((R, D), BF16), ((R, 1024), BF16), ((R, 1024), BF16), ((F, 256), F32))
    local = pl.BlockSpec(memory_space=pltpu.VMEM)
    held = pl.pallas_call(
        kernel,
        name="attention_back",
        out_shape=tuple(vm(shape, dtype) for shape, dtype in shapes),
        in_specs=[hbm] * 5 + [pl.BlockSpec(memory_space=pltpu.SMEM)],
        out_specs=(local,) * 4,
        scratch_shapes=scratch,
        compiler_params=pltpu.CompilerParams(
            collective_id=0, has_side_effects=True, vmem_limit_bytes=60 * 1024 * 1024
        ),
    )(grad_out[0], queries[0], keys[0], values[0], out_weight, doc_starts)
    out = pl.pallas_call(
        write_out,
        name="write_out",
        out_shape=tuple(jax.ShapeDtypeStruct(shape, dtype) for shape, dtype in shapes),
        in_specs=[local] * 4,
        out_specs=(hbm,) * 4,
        scratch_shapes=[dma((4,))],
    )(*[pltpu.with_memory_space_constraint(x, pltpu.VMEM) for x in held])
    return (out[0][None], out[1][None], out[2][None], out[3])


def solution(mesh):
    return jax.shard_map(
        body,
        mesh=mesh,
        in_specs=(
            P("dp", "seq", None),
            P("dp", "seq", None),
            P("dp", "seq", None),
            P("dp", "seq", None),
            P("seq", None),
            P("dp", None),
        ),
        out_specs=(
            P("dp", "seq", None),
            P("dp", "seq", None),
            P("dp", "seq", None),
            P("seq", "dp"),
        ),
        check_vma=False,
    )
```

time: 104 us -> 86.6 us (0.83)
  Pallas kernels: 95.2 us -> 85.6 us
  local copies, waits for them, and re-layouts: 7.49 us -> 0 us
    pallas_call x1 -> x2, Pallas kernels: 95.2 us -> 85.6 us  [the longest x1 84.3 us: body(): pl.pallas_call(kernel, name='attention_back', out_shape=tuple((vm(shape,...]
    unnamed x4 -> x0, local copies, waits for them, and re-layouts: 7.49 us -> none
where the time goes in v2:
time: 86.6 us; the launch traced here: 86.5 us
  Pallas kernels  85.6 us (99%)
    pallas_call x1, Pallas kernels, body(): pl.pallas_call(kernel, name='attention_back', out_shape=tuple((vm(shape,...  84.3 us

profile of v2, /device:TPU:1, one launch (start us, length us, event | category | flops | bytes accessed | tf_op | source)
XLA Modules:
  0.0 86.5 jit_solution(3969826098970272456)
XLA Ops:
  0.6 84.3 %attention_back.1 = (bf16[128,4096]{1,0:T(8,128)(2,1)S(1)}, bf16[128,1024]{1,0:T(8,128)(2,1)S(1)}, bf16[128,1024]{1,0:T(8,128)(2,1)S(1)}, f32[512,256]{1,0:T(8,128)S(1)}) custom-call(bf16[128,4096]{1,0:T(8,128)(2,1)} %bitcast.7, bf16[128,4096]{1,0:T(8,128)(2,1)} %bitcast.8, bf16[128,1024]{1,0:T(8,128)(2,1)} %bitcast.9, bf16[128,1024]{1,0:T(8,128)(2,1)} %bitcast.10, ...), custom_call_target="tpu_custom_call" | custom-call | tf_op jit(solution)/shard_map/attention_back/pallas_call | solution.py:458
  84.9 1.3 %write_out.1 = (bf16[128,4096]{1,0:T(8,128)(2,1)}, bf16[128,1024]{1,0:T(8,128)(2,1)}, bf16[128,1024]{1,0:T(8,128)(2,1)}, f32[512,256]{1,0:T(8,128)}) custom-call(bf16[128,4096]{1,0:T(8,128)(2,1)S(1)} %get-tuple-element.12.a, bf16[128,1024]{1,0:T(8,128)(2,1)S(1)} %get-tuple-element.13.b, bf16[128,1024]{1,0:T(8,128)(2,1)S(1)} %get-tuple-element.14.c, ...), custom_call_target="tpu_custom_call" | custom-call | tf_op jit(solution)/shard_map/write_out/pallas_call | solution.py:469

commit v3 on v2

--- a/solution.py
+++ b/solution.py
@@ -12,6 +12,8 @@
 BF16 = jnp.bfloat16
 T = 1024
 R = 128
+XR = 320
+ZR = 512 - XR
 H = 4
 DH = 128
 F = H * DH
@@ -21,7 +23,7 @@
 NC = 8
 CW = D // NC
 CHUNK_X = (2, 2, 1, 3, 1, 3, 0, 0)
-EARLY = 2
+EARLY = 3
 CHUNK_OWN = (0, 1, 0, 0, 1, 1, 0, 1)
 SCALE = 1.0 / math.sqrt(DH)
 NT = (((1,), (1,)), ((), ()))
@@ -46,7 +48,7 @@
     dqs, dKa, dVa, dkb, dvb,
     s_q, r_q, s_k, r_k, s_v, r_v, l_q, l_k, l_v,
     s_ag, r_m, r_p, r_o, r_own, r_near, r_opp, l_g, l_w,
-    s_x, r_x, s_z, s_x2, r_x2, s_z2, r_z2, r_z,
+    s_x, s_z, s_x2, r_x2, s_z2, r_z2, r_x, r_z,
     s_dq, r_dq, s_dk, r_dk, s_dv, r_dv, l_dq, l_dk, l_dv,
 ):
     dp = lax.axis_index("dp")
@@ -200,7 +202,10 @@
 
     hc = [pl.ds(h * DH, DH) for h in range(H)]
 
-    def backward(b):
+    my_f = pl.ds(mult(me * F, F), F)
+    my_d = pl.ds(mult(me * DH, DH), DH)
+
+    def backward(b, far=True):
         rows = block_of(b)
 
         def pair(n, g):
@@ -217,6 +222,12 @@
                 gs.append(grad)
                 dss.append(ds)
             dVa[:n] += dot(jnp.concatenate(ps, axis=1), jnp.concatenate(gs, axis=0))
+            for c in range(2 if far else 0):
+                remote(
+                    dqs.at[b, pl.ds(c * R, R), pl.ds(mult(g * B, B), B)],
+                    dq_o.at[:, pl.ds(mult(me * F + g * B, B), B)],
+                    s_dq, r_dq, seq_dev(b * 2 + c),
+                ).start()
             qq = jnp.concatenate([qs[rows, c] for c in cols], axis=0)
             dKa[:n] += dot(jnp.concatenate(dss, axis=1), qq)
 
@@ -228,16 +239,7 @@
                 def _(g):
                     pair((i + 1) * B, g)
 
-    my_f = pl.ds(mult(me * F, F), F)
-    my_d = pl.ds(mult(me * DH, DH), DH)
-
-    def send_dq(b):
-        for c in range(2):
-            remote(
-                dqs.at[b, pl.ds(c * R, R)], dq_o.at[:, my_f], s_dq, r_dq, seq_dev(b * 2 + c)
-            ).start()
-
-    backward(Y)
+    backward(Y, False)
     other_rows = pl.ds(mult((1 - C) * R, R), R)
     own_rows = pl.ds(mult(C * R, R), R)
     remote(dqs.at[Y, other_rows], dq_o.at[:, my_f], s_dq, r_dq, sib).start()
@@ -262,7 +264,7 @@
         dx = CHUNK_X[j]
         if dx:
             remote(
-                Wb.at[j, pl.ds(0, 256)], rx.at[dx - 1, CHUNK_OWN[j]], s_x, r_x,
+                Wb.at[j, pl.ds(0, XR)], rx.at[CHUNK_OWN[j], dx - 1], s_x, r_x.at[CHUNK_OWN[j]],
                 grid_dev(lax.rem(X + dx, 4), Z),
             ).start()
         if CHUNK_OWN[j]:
@@ -271,7 +273,7 @@
             sends = [(c * 256, 2 * other + c) for c in range(2)]
         for col, zz in sends:
             remote(
-                Wb.at[j, pl.ds(256, 256), pl.ds(col, 256)], rz.at[dx, z_slot(zz)], s_z, r_z.at[dx],
+                Wb.at[j, pl.ds(XR, ZR), pl.ds(col, 256)], rz.at[dx, z_slot(zz)], s_z, r_z.at[dx],
                 grid_dev(X, zz),
             ).start()
 
@@ -281,7 +283,7 @@
         for b in (Y, y_up, y_down):
             d = dot(OT[:, block_of(b)], G[j, block_of(b)])
             s = d if s is None else s + d
-        Wacc[j - 2] = s
+        Wacc[j - EARLY] = s
         for b in (y_up, y_down):
             project(j, b, False)
 
@@ -296,51 +298,66 @@
     def finish(j):
         arrived(j, y_opp * 2 + 1 - C, r_opp.at[j])
         project(j, y_opp, False)
-        Wb[j] = (Wacc[j - 2] + dot(OT[:, block_of(y_opp)], G[j, block_of(y_opp)])).astype(BF16)
+        Wb[j] = (Wacc[j - EARLY] + dot(OT[:, block_of(y_opp)], G[j, block_of(y_opp)])).astype(BF16)
         scatter(j)
 
-    relay(2)
     relay(3)
     opposite(0)
     full(0)
     opposite(1)
     relay(4)
-    near(2)
+    near(3)
     full(1)
     relay(5)
-    near(3)
     near(4)
+    opposite(2)
+    near(5)
+    full(2)
     relay(6)
-    near(5)
+    near(6)
     relay(7)
-    near(6)
     near(7)
     projected(y_up)
     projected(y_down)
-    opposite(2)
     opposite(3)
     backward(y_up)
-    send_dq(y_up)
-    finish(2)
     finish(3)
     opposite(4)
     opposite(5)
+    finish(4)
+    finish(5)
     backward(y_down)
-    send_dq(y_down)
     opposite(6)
     opposite(7)
-    for j in range(4, NC):
-        finish(j)
+    finish(6)
+    finish(7)
     projected(y_opp)
+
+    def send_kv(kb):
+        rows = pl.ds(kb * B, B)
+        dkb[rows] = (dKa[rows] * SCALE).astype(BF16)
+        dvb[rows] = dVa[rows].astype(BF16)
+        for c in range(2):
+            g = kb * 2 + c
+
+            @pl.when(me != g)
+            def _():
+                remote(dkb.at[rows_of(g)], dk_o.at[:, my_d], s_dk, r_dk, seq_dev(g)).start()
+                remote(dvb.at[rows_of(g)], dv_o.at[:, my_d], s_dv, r_dv, seq_dev(g)).start()
+
+    for kb in range(1, NB):
+
+        @pl.when((kb > y_opp) & (kb != Y))
+        def _():
+            send_kv(kb)
+
     backward(y_opp)
-    send_dq(y_opp)
-
-    dkb[...] = (dKa[...] * SCALE).astype(BF16)
-    dvb[...] = dVa[...].astype(BF16)
-    for o in (4, 5, 3, 2, 6, 1, 7):
-        g = lax.rem(me + o, 8)
-        remote(dkb.at[rows_of(g)], dk_o.at[:, my_d], s_dk, r_dk, seq_dev(g)).start()
-        remote(dvb.at[rows_of(g)], dv_o.at[:, my_d], s_dv, r_dv, seq_dev(g)).start()
+    for kb in range(NB):
+
+        @pl.when((kb <= y_opp) | (kb == Y))
+        def _():
+            send_kv(kb)
+
     own_dk = pltpu.make_async_copy(dkb.at[my_rows], dk_o.at[:, my_d], l_dk)
     own_dv = pltpu.make_async_copy(dvb.at[my_rows], dv_o.at[:, my_d], l_dv)
     own_dk.start()
@@ -351,7 +368,7 @@
 
     def z_sum(dx):
         pltpu.make_async_copy(rz.at[dx], rz.at[dx], r_z.at[dx]).wait()
-        s = Wb[chunk_at[dx, 1], 256:, own_cols].astype(F32)
+        s = Wb[chunk_at[dx, 1], XR:, own_cols].astype(F32)
         for i in range(3):
             s += rz[dx, i].astype(F32)
         if dx:
@@ -362,34 +379,38 @@
         else:
             fin[...] = s
 
+    def x_sum(e):
+        pltpu.make_async_copy(rx.at[e], rx.at[e], r_x.at[e]).wait()
+        s = Wb[chunk_at[0, e], :XR].astype(F32)
+        for i in range(3):
+            s += rx[e, i].astype(F32)
+        s1b[e] = s.astype(BF16)
+        if e:
+            sends = [(mult((1 - par) * 256, 256), Z + 1 - 2 * par)]
+        else:
+            sends = [(c * 256, 2 * other + c) for c in range(2)]
+        for col, zz in sends:
+            remote(
+                s1b.at[e, :, pl.ds(col, 256)], rx2.at[z_slot(zz)], s_x2, r_x2, grid_dev(X, zz)
+            ).start()
+
     z_sum(2)
+    x_sum(0)
     z_sum(1)
     z_sum(3)
-    pltpu.make_async_copy(rx, rx, r_x).wait()
-    for e in range(2):
-        s = Wb[chunk_at[0, e], :256].astype(F32)
-        for i in range(3):
-            s += rx[i, e].astype(F32)
-        s1b[e] = s.astype(BF16)
-    x_sends = [(0, c * 256, 2 * other + c) for c in range(2)]
-    x_sends.append((1, mult((1 - par) * 256, 256), Z + 1 - 2 * par))
-    for e, col, zz in x_sends:
-        remote(
-            s1b.at[e, :, pl.ds(col, 256)], rx2.at[z_slot(zz)], s_x2, r_x2, grid_dev(X, zz)
-        ).start()
-
+    x_sum(1)
     z_sum(0)
     pltpu.make_async_copy(rx2, rx2, r_x2).wait()
     norm = 1.0 / math.sqrt(T * 16)
     s = s1b[1, :, own_cols].astype(F32)
     for i in range(3):
         s += rx2[i].astype(F32)
-    wg_o[:256] = s * norm
+    wg_o[:XR] = s * norm
     pltpu.make_async_copy(rz2, rz2, r_z2).wait()
     s = fin[...]
     for i in range(3):
         s += rz2[i].astype(F32)
-    wg_o[256:] = s * norm
+    wg_o[XR:] = s * norm
 
     def drain(ref, *sems):
         for sem in sems:
@@ -403,7 +424,8 @@
     drain(G.at[pl.ds(0, 7)], s_ag)
     drain(rx, s_x)
     drain(rz, s_z)
-    drain(rx2, s_x2, s_z2)
+    drain(rx2, s_x2)
+    drain(rz2, s_z2)
 
 
 def write_out(a, b, c, d, ao, bo, co, do, sem):
@@ -434,15 +456,15 @@
         vm((NB, T, B), F32),
         vm((T, F), F32),
         vm((T, F), BF16),
-        vm((NC - 2, F, CW), F32),
+        vm((NC - EARLY, F, CW), F32),
         vm((NC, F, CW), BF16),
-        vm((3, 2, 256, 512), BF16),
-        vm((4, 3, 256, 256), BF16),
-        vm((2, 256, 512), BF16),
-        vm((3, 256, 256), BF16),
-        vm((3, 256, 256), BF16),
-        vm((3, 256, 256), BF16),
-        vm((256, 256), F32),
+        vm((2, 3, XR, 512), BF16),
+        vm((4, 3, ZR, 256), BF16),
+        vm((2, XR, 512), BF16),
+        vm((3, ZR, 256), BF16),
+        vm((3, XR, 256), BF16),
+        vm((3, ZR, 256), BF16),
+        vm((ZR, 256), F32),
         vm((NB, B, F), BF16),
         vm((T, DH), F32),
         vm((T, DH), F32),
@@ -451,7 +473,7 @@
     ]
     scratch += [dma] * 9
     scratch += [dma] + [dma((NC,))] * 6 + [dma] * 2
-    scratch += [dma] * 7 + [dma((4,))]
+    scratch += [dma] * 6 + [dma((2,)), dma((4,))]
     scratch += [dma] * 9
     shapes = (((R, D), BF16), ((R, 1024), BF16), ((R, 1024), BF16), ((F, 256), F32))
     local = pl.BlockSpec(memory_space=pltpu.VMEM)

time: 86.6 us -> 85.6 us (0.988)
  Pallas kernels: 85.6 us -> 84.6 us
    pallas_call x1, Pallas kernels: 84.3 us -> 83.3 us  [body(): pl.pallas_call(kernel, name='attention_back', out_shape=tuple((vm(shape,...]
where the time goes in v3:
time: 85.6 us; the launch traced here: 85.5 us
  Pallas kernels  84.6 us (99%)
    pallas_call x1, Pallas kernels, body(): pl.pallas_call(kernel, name='attention_back', out_shape=tuple((vm(shape,...  83.3 us

profile of v3, /device:TPU:1, one launch (start us, length us, event | category | flops | bytes accessed | tf_op | source)
XLA Modules:
  0.0 85.5 jit_solution(2836798043281014411)
XLA Ops:
  0.6 83.3 %attention_back.1 = (bf16[128,4096]{1,0:T(8,128)(2,1)S(1)}, bf16[128,1024]{1,0:T(8,128)(2,1)S(1)}, bf16[128,1024]{1,0:T(8,128)(2,1)S(1)}, f32[512,256]{1,0:T(8,128)S(1)}) custom-call(bf16[128,4096]{1,0:T(8,128)(2,1)} %bitcast.7, bf16[128,4096]{1,0:T(8,128)(2,1)} %bitcast.8, bf16[128,1024]{1,0:T(8,128)(2,1)} %bitcast.9, bf16[128,1024]{1,0:T(8,128)(2,1)} %bitcast.10, ...), custom_call_target="tpu_custom_call" | custom-call | tf_op jit(solution)/shard_map/attention_back/pallas_call | solution.py:480
  83.9 1.3 %write_out.1 = (bf16[128,4096]{1,0:T(8,128)(2,1)}, bf16[128,1024]{1,0:T(8,128)(2,1)}, bf16[128,1024]{1,0:T(8,128)(2,1)}, f32[512,256]{1,0:T(8,128)}) custom-call(bf16[128,4096]{1,0:T(8,128)(2,1)S(1)} %get-tuple-element.12.a, bf16[128,1024]{1,0:T(8,128)(2,1)S(1)} %get-tuple-element.13.b, bf16[128,1024]{1,0:T(8,128)(2,1)S(1)} %get-tuple-element.14.c, ...), custom_call_target="tpu_custom_call" | custom-call | tf_op jit(solution)/shard_map/write_out/pallas_call | solution.py:491

commit v4 on v3

--- a/solution.py
+++ b/solution.py
@@ -23,7 +23,7 @@
 NC = 8
 CW = D // NC
 CHUNK_X = (2, 2, 1, 3, 1, 3, 0, 0)
-EARLY = 3
+EARLY = 4
 CHUNK_OWN = (0, 1, 0, 0, 1, 1, 0, 1)
 SCALE = 1.0 / math.sqrt(DH)
 NT = (((1,), (1,)), ((), ()))
@@ -301,27 +301,25 @@
         Wb[j] = (Wacc[j - EARLY] + dot(OT[:, block_of(y_opp)], G[j, block_of(y_opp)])).astype(BF16)
         scatter(j)
 
-    relay(3)
     opposite(0)
     full(0)
+    relay(4)
     opposite(1)
-    relay(4)
-    near(3)
+    near(4)
     full(1)
     relay(5)
-    near(4)
+    near(5)
     opposite(2)
-    near(5)
     full(2)
     relay(6)
+    opposite(3)
     near(6)
+    full(3)
     relay(7)
     near(7)
     projected(y_up)
     projected(y_down)
-    opposite(3)
     backward(y_up)
-    finish(3)
     opposite(4)
     opposite(5)
     finish(4)

time: 85.6 us -> 85.3 us (level)
  no operation moved by 1% of the time
where the time goes in v4:
time: 85.3 us; the launch traced here: 85.2 us
  Pallas kernels  84.4 us (99%)
    pallas_call x1, Pallas kernels, body(): pl.pallas_call(kernel, name='attention_back', out_shape=tuple((vm(shape,...  83 us

profile of v4, /device:TPU:1, one launch (start us, length us, event | category | flops | bytes accessed | tf_op | source)
XLA Modules:
  0.0 85.2 jit_solution(7917274396354896813)
XLA Ops:
  0.6 83.0 %attention_back.1 = (bf16[128,4096]{1,0:T(8,128)(2,1)S(1)}, bf16[128,1024]{1,0:T(8,128)(2,1)S(1)}, bf16[128,1024]{1,0:T(8,128)(2,1)S(1)}, f32[512,256]{1,0:T(8,128)S(1)}) custom-call(bf16[128,4096]{1,0:T(8,128)(2,1)} %bitcast.7, bf16[128,4096]{1,0:T(8,128)(2,1)} %bitcast.8, bf16[128,1024]{1,0:T(8,128)(2,1)} %bitcast.9, bf16[128,1024]{1,0:T(8,128)(2,1)} %bitcast.10, ...), custom_call_target="tpu_custom_call" | custom-call | tf_op jit(solution)/shard_map/attention_back/pallas_call | solution.py:478
  83.7 1.3 %write_out.1 = (bf16[128,4096]{1,0:T(8,128)(2,1)}, bf16[128,1024]{1,0:T(8,128)(2,1)}, bf16[128,1024]{1,0:T(8,128)(2,1)}, f32[512,256]{1,0:T(8,128)}) custom-call(bf16[128,4096]{1,0:T(8,128)(2,1)S(1)} %get-tuple-element.12.a, bf16[128,1024]{1,0:T(8,128)(2,1)S(1)} %get-tuple-element.13.b, bf16[128,1024]{1,0:T(8,128)(2,1)S(1)} %get-tuple-element.14.c, ...), custom_call_target="tpu_custom_call" | custom-call | tf_op jit(solution)/shard_map/write_out/pallas_call | solution.py:489

commit v5 on v3

--- a/solution.py
+++ b/solution.py
@@ -23,7 +23,7 @@
 NC = 8
 CW = D // NC
 CHUNK_X = (2, 2, 1, 3, 1, 3, 0, 0)
-EARLY = 3
+EARLY = 2
 CHUNK_OWN = (0, 1, 0, 0, 1, 1, 0, 1)
 SCALE = 1.0 / math.sqrt(DH)
 NT = (((1,), (1,)), ((), ()))
@@ -301,38 +301,37 @@
         Wb[j] = (Wacc[j - EARLY] + dot(OT[:, block_of(y_opp)], G[j, block_of(y_opp)])).astype(BF16)
         scatter(j)
 
+    relay(2)
     relay(3)
     opposite(0)
     full(0)
     opposite(1)
     relay(4)
-    near(3)
+    near(2)
     full(1)
     relay(5)
+    near(3)
     near(4)
-    opposite(2)
+    relay(6)
     near(5)
-    full(2)
-    relay(6)
+    relay(7)
     near(6)
-    relay(7)
     near(7)
     projected(y_up)
     projected(y_down)
+    opposite(2)
     opposite(3)
     backward(y_up)
+    finish(2)
     finish(3)
     opposite(4)
     opposite(5)
-    finish(4)
-    finish(5)
     backward(y_down)
     opposite(6)
     opposite(7)
-    finish(6)
-    finish(7)
+    for j in range(4, NC):
+        finish(j)
     projected(y_opp)
-
     def send_kv(kb):
         rows = pl.ds(kb * B, B)
         dkb[rows] = (dKa[rows] * SCALE).astype(BF16)

time: 85.6 us -> 84.7 us (0.989)
  Pallas kernels: 84.6 us -> 83.1 us
    pallas_call x1, Pallas kernels: 83.3 us -> 81.8 us  [body(): pl.pallas_call(kernel, name='attention_back', out_shape=tuple((vm(shape,...]
where the time goes in v5:
time: 84.7 us; the launch traced here: 84 us
  Pallas kernels  83.1 us (98%)
    pallas_call x1, Pallas kernels, body(): pl.pallas_call(kernel, name='attention_back', out_shape=tuple((vm(shape,...  81.8 us

profile of v5, /device:TPU:1, one launch (start us, length us, event | category | flops | bytes accessed | tf_op | source)
XLA Modules:
  0.0 84.0 jit_solution(7988440216141566727)
XLA Ops:
  0.6 81.8 %attention_back.1 = (bf16[128,4096]{1,0:T(8,128)(2,1)S(1)}, bf16[128,1024]{1,0:T(8,128)(2,1)S(1)}, bf16[128,1024]{1,0:T(8,128)(2,1)S(1)}, f32[512,256]{1,0:T(8,128)S(1)}) custom-call(bf16[128,4096]{1,0:T(8,128)(2,1)} %bitcast.7, bf16[128,4096]{1,0:T(8,128)(2,1)} %bitcast.8, bf16[128,1024]{1,0:T(8,128)(2,1)} %bitcast.9, bf16[128,1024]{1,0:T(8,128)(2,1)} %bitcast.10, ...), custom_call_target="tpu_custom_call" | custom-call | tf_op jit(solution)/shard_map/attention_back/pallas_call | solution.py:479
  82.4 1.3 %write_out.1 = (bf16[128,4096]{1,0:T(8,128)(2,1)}, bf16[128,1024]{1,0:T(8,128)(2,1)}, bf16[128,1024]{1,0:T(8,128)(2,1)}, f32[512,256]{1,0:T(8,128)}) custom-call(bf16[128,4096]{1,0:T(8,128)(2,1)S(1)} %get-tuple-element.12.a, bf16[128,1024]{1,0:T(8,128)(2,1)S(1)} %get-tuple-element.13.b, bf16[128,1024]{1,0:T(8,128)(2,1)S(1)} %get-tuple-element.14.c, ...), custom_call_target="tpu_custom_call" | custom-call | tf_op jit(solution)/shard_map/write_out/pallas_call | solution.py:490

commit v6 on v5

--- a/solution.py
+++ b/solution.py
@@ -12,7 +12,7 @@
 BF16 = jnp.bfloat16
 T = 1024
 R = 128
-XR = 320
+XR = 352
 ZR = 512 - XR
 H = 4
 DH = 128

time: 84.7 us -> 86.1 us (1.017)
  Pallas kernels: 83.1 us -> 85.2 us
    pallas_call x1, Pallas kernels: 81.8 us -> 83.8 us  [body(): pl.pallas_call(kernel, name='attention_back', out_shape=tuple((vm(shape,...]
where the time goes in v6:
time: 86.1 us; the launch traced here: 86 us
  Pallas kernels  85.2 us (99%)
    pallas_call x1, Pallas kernels, body(): pl.pallas_call(kernel, name='attention_back', out_shape=tuple((vm(shape,...  83.8 us

profile of v6, /device:TPU:1, one launch (start us, length us, event | category | flops | bytes accessed | tf_op | source)
XLA Modules:
  0.0 86.0 jit_solution(3701353362285755727)
XLA Ops:
  0.6 83.8 %attention_back.1 = (bf16[128,4096]{1,0:T(8,128)(2,1)S(1)}, bf16[128,1024]{1,0:T(8,128)(2,1)S(1)}, bf16[128,1024]{1,0:T(8,128)(2,1)S(1)}, f32[512,256]{1,0:T(8,128)S(1)}) custom-call(bf16[128,4096]{1,0:T(8,128)(2,1)} %bitcast.7, bf16[128,4096]{1,0:T(8,128)(2,1)} %bitcast.8, bf16[128,1024]{1,0:T(8,128)(2,1)} %bitcast.9, bf16[128,1024]{1,0:T(8,128)(2,1)} %bitcast.10, ...), custom_call_target="tpu_custom_call" | custom-call | tf_op jit(solution)/shard_map/attention_back/pallas_call | solution.py:479
  84.5 1.3 %write_out.1 = (bf16[128,4096]{1,0:T(8,128)(2,1)}, bf16[128,1024]{1,0:T(8,128)(2,1)}, bf16[128,1024]{1,0:T(8,128)(2,1)}, f32[512,256]{1,0:T(8,128)}) custom-call(bf16[128,4096]{1,0:T(8,128)(2,1)S(1)} %get-tuple-element.12.a, bf16[128,1024]{1,0:T(8,128)(2,1)S(1)} %get-tuple-element.13.b, bf16[128,1024]{1,0:T(8,128)(2,1)S(1)} %get-tuple-element.14.c, ...), custom_call_target="tpu_custom_call" | custom-call | tf_op jit(solution)/shard_map/write_out/pallas_call | solution.py:490
